TPU v7x, 256 devices: a whole 4x4x8 slice. The times are simulated.
256 devices in a mesh: req: 32 (over x, y, core), tp: 8 (over z).
Axes of the slice: x: 4, y: 4, z: 8, core: 2. Of those that a mesh axis runs over, the one named last changes fastest.
Arguments:
- queries: bfloat16 [4096, 8192], P('req', 'tp'), may hold values from -80 to 80
- incoming_key_value: bfloat16 [2, 4096, 1024], P(None, 'req', 'tp'), may hold values from -4 to 4
- key_value_pages: bfloat16 [16384, 32, 2, 1024], P('req', None, None, 'tp'), may hold values from -4 to 4
- page_request_home: int32 [16384], P('req'), may hold values from 0 to 16383, as said below
- lengths: int32 [1024], P('req'), may hold values from 1 to 512, 262144 in all
- request_adapter_index: int32 [1024], P('req'), may hold values from 0 to 63
- adapter_storage_slot: int32 [64], replicated, may hold values from 0 to 63, each once
- adapter_down_factor: bfloat16 [64, 8192, 64], P('req', 'tp'), may hold values from -0.25 to 0.25
- adapter_up_factor: bfloat16 [64, 64, 8192], P('req'), may hold values from -0.75 to 0.75
- output_projection_weight: bfloat16 [8192, 8192], P('tp', 'req'), may hold values from -0.75 to 0.75
Outputs:
- attn_out: bfloat16 [4096, 8192], P('tp', 'req')
Inputs may be any that keep to these rules, and one draw needn't show every extreme that they name: `page_request_home`: each value once. Pages p with p // 512 = a hold pages of requests i with i // 32 = b, b != a, for at most 2 pages p for every pair a, b; in every draw some a holds exactly 2 pages of every b != a.
All inputs are finite; a program needn't handle non-finite values. No bound on the sum of `lengths` on one device may be relied on, other than what follows from the above.
Results may differ from a plain program's by a relative error of at most 0.0058.
Values may be sent and summed in bfloat16 or wider, within the bound.
A program may use at most 128 MiB of HBM per device.

v0:
```python
import math

import jax
import jax.numpy as jnp
from jax import lax
from jax.sharding import PartitionSpec as P

QUERY_HEADS = 64
KEY_VALUE_HEADS = 8
HEAD_WIDTH = 128
STEP_COUNT = 4
PAGE_LENGTH = 32
MAXP = 16
CAP = 2


def relocate(key_value_pages, page_request_home, my_req, req_count):
    per_dev = key_value_pages.shape[0]
    destination = page_request_home // per_dev
    remote = destination != my_req
    matches = (destination[:, None] == jnp.arange(req_count, dtype=jnp.int32)[None, :]) & remote[
        :, None
    ]
    before = jnp.cumsum(matches.astype(jnp.int32), axis=0) - 1
    placing = jnp.sum(jnp.where(matches, before, 0), axis=1)
    target = jnp.where(remote, destination * CAP + placing, req_count * CAP)
    page_numbers = jnp.arange(per_dev, dtype=jnp.int32)
    out_match = target[:, None] == jnp.arange(req_count * CAP, dtype=jnp.int32)[None, :]
    filled = jnp.any(out_match, axis=0)
    out_source = jnp.sum(jnp.where(out_match, page_numbers[:, None], 0), axis=0)
    out_label = jnp.sum(jnp.where(out_match, page_request_home[:, None], 0), axis=0)
    picked = jnp.take(key_value_pages, out_source, axis=0)
    outbox = jnp.where(filled[:, None, None, None], picked, jnp.zeros((), key_value_pages.dtype))
    labels = jnp.where(filled, out_label, -1)
    inbox_pages, arrived = (
        lax.all_to_all(outbox, "req", split_axis=0, concat_axis=0, tiled=True),
        lax.all_to_all(labels, "req", split_axis=0, concat_axis=0, tiled=True),
    )
    own_label = jnp.where(remote, -1, page_request_home - my_req * per_dev)
    in_label = jnp.where(arrived >= 0, arrived - my_req * per_dev, -1)
    candidate_label = jnp.concatenate([own_label, in_label], axis=0)
    candidates = jnp.concatenate([key_value_pages, inbox_pages], axis=0)
    candidate_numbers = jnp.arange(candidate_label.shape[0], dtype=jnp.int32)
    slot_match = candidate_label[:, None] == page_numbers[None, :]
    slot_source = jnp.sum(jnp.where(slot_match, candidate_numbers[:, None], 0), axis=0)
    return jnp.take(candidates, slot_source, axis=0)


def attend(queries, incoming_key_value, cache_pages, lengths):
    heads_kv = cache_pages.shape[-1] // HEAD_WIDTH
    query_group_count = QUERY_HEADS // KEY_VALUE_HEADS
    requests = lengths.shape[0]
    cache_extent = MAXP * PAGE_LENGTH
    score_scale = 1.0 / math.sqrt(HEAD_WIDTH)
    stored_entries = cache_pages.reshape(requests, cache_extent, 2, heads_kv, HEAD_WIDTH)
    fresh_key_value = incoming_key_value.reshape(2, requests, STEP_COUNT, heads_kv, HEAD_WIDTH)
    query_vectors = queries.reshape(requests, STEP_COUNT, heads_kv, query_group_count, HEAD_WIDTH)
    old_scores = (
        jnp.einsum(
            "rsgqd,rlgd->rgqsl",
            query_vectors,
            stored_entries[:, :, 0],
            preferred_element_type=jnp.float32,
        )
        * score_scale
    )
    new_scores = (
        jnp.einsum(
            "rsgqd,rtgd->rgqst",
            query_vectors,
            fresh_key_value[0],
            preferred_element_type=jnp.float32,
        )
        * score_scale
    )
    keep_old = jnp.arange(cache_extent, dtype=jnp.int32)[None, :] < lengths[:, None]
    keep_new = jnp.arange(STEP_COUNT)[None, :] <= jnp.arange(STEP_COUNT)[:, None]
    old_scores = jnp.where(keep_old[:, None, None, None, :], old_scores, -jnp.inf)
    new_scores = jnp.where(keep_new[None, None, None], new_scores, -jnp.inf)
    row_top = jnp.maximum(jnp.max(old_scores, axis=-1), jnp.max(new_scores, axis=-1))
    old_weights = jnp.exp(old_scores - row_top[..., None])
    new_weights = jnp.exp(new_scores - row_top[..., None])
    totals = jnp.sum(old_weights, axis=-1) + jnp.sum(new_weights, axis=-1)
    old_probs = (old_weights / totals[..., None]).astype(jnp.bfloat16)
    new_probs = (new_weights / totals[..., None]).astype(jnp.bfloat16)
    attention_mixed_output = jnp.einsum(
        "rgqsl,rlgd->rsgqd", old_probs, stored_entries[:, :, 1], preferred_element_type=jnp.float32
    )
    attention_mixed_output = attention_mixed_output + jnp.einsum(
        "rgqst,rtgd->rsgqd", new_probs, fresh_key_value[1], preferred_element_type=jnp.float32
    )
    return attention_mixed_output.astype(jnp.bfloat16).reshape(
        requests * STEP_COUNT, heads_kv * query_group_count * HEAD_WIDTH
    )


def on_device(
    queries,
    incoming_key_value,
    key_value_pages,
    page_request_home,
    lengths,
    request_adapter_index,
    adapter_storage_slot,
    adapter_down_factor,
    adapter_up_factor,
    output_projection_weight,
):
    req_count = lax.axis_size("req")
    tp_count = lax.axis_size("tp")
    my_req = lax.axis_index("req")
    my_lane = lax.axis_index("tp")
    cache_pages = relocate(key_value_pages, page_request_home, my_req, req_count)
    attention_mixed_output = attend(queries, incoming_key_value, cache_pages, lengths)
    own_tokens = attention_mixed_output.shape[0]
    everyone, adapters = (
        lax.all_gather(attention_mixed_output, "req", axis=0, tiled=True),
        lax.all_gather(request_adapter_index, "req", axis=0, tiled=True),
    )
    slot_count = adapter_storage_slot.shape[0]
    match_table = adapters[:, None] == jnp.arange(slot_count, dtype=jnp.int32)[None, :]
    req_slot = jnp.sum(jnp.where(match_table, adapter_storage_slot[None, :], 0), axis=1)
    token_slot = jnp.repeat(req_slot, STEP_COUNT)
    block_rows = everyone.shape[0] // tp_count
    plain_output_rows = lax.psum_scatter(
        jnp.dot(everyone, output_projection_weight, preferred_element_type=jnp.float32),
        "tp",
        scatter_dimension=0,
        tiled=True,
    )
    gathered_down_factors = lax.all_gather(adapter_down_factor, "req", axis=0, tiled=True)
    local_reduced_rows = jnp.einsum(
        "td,adr->tar",
        attention_mixed_output,
        gathered_down_factors,
        preferred_element_type=jnp.float32,
    )
    own_slot = lax.dynamic_slice_in_dim(token_slot, my_req * own_tokens, own_tokens)
    selected_pages = own_slot[:, None] == jnp.arange(slot_count, dtype=jnp.int32)[None, :]
    adapter_partial = jnp.sum(
        jnp.where(selected_pages[:, :, None], local_reduced_rows, 0.0), axis=1
    )
    distributed_terms = lax.all_gather(adapter_partial, "req", axis=0, tiled=True)
    low_rows = lax.psum_scatter(distributed_terms, "tp", scatter_dimension=0, tiled=True)
    up_factor_columns = lax.all_to_all(
        adapter_up_factor, "req", split_axis=2, concat_axis=0, tiled=True
    )
    low_bf = low_rows.astype(jnp.bfloat16)
    block_slot = lax.dynamic_slice_in_dim(token_slot, my_lane * block_rows, block_rows)
    selector = (block_slot[:, None] == jnp.arange(slot_count, dtype=jnp.int32)[None, :]).astype(
        jnp.bfloat16
    )
    expanded = (selector[:, :, None] * low_bf[:, None, :]).reshape(
        block_rows, slot_count * up_factor_columns.shape[1]
    )
    adapter_output_rows = jnp.dot(
        expanded,
        up_factor_columns.reshape(
            slot_count * up_factor_columns.shape[1], up_factor_columns.shape[2]
        ),
        preferred_element_type=jnp.float32,
    )
    return (plain_output_rows + adapter_output_rows).astype(jnp.bfloat16)


def solution(mesh):
    return jax.shard_map(
        on_device,
        mesh=mesh,
        in_specs=(
            P("req", "tp"),
            P(None, "req", "tp"),
            P("req", None, None, "tp"),
            P("req"),
            P("req"),
            P("req"),
            P(),
            P("req", "tp", None),
            P("req", None, None),
            P("tp", "req"),
        ),
        out_specs=P("tp", "req"),
        check_vma=False,
    )
```

profile of v0, /device:TPU:1, one launch (start us, length us, event | category | flops | bytes accessed | tf_op | source)
XLA Modules:
  0.0 376.8 jit_solution(3903700811539374699)
XLA Ops:
  11.2 8.6 %all-to-all-start = ((s32[32,2,1]{1,2,0:T(1,128)}), s32[32,2,1]{1,2,0:T(1,128)S(1)}, u32[]{:S(2)}, u32[]{:S(2)}) async-start(s32[32,2,1]{1,2,0:T(1,128)} %bitcast.3), calls=%async_computation | async-start | bytes 32768 | tf_op jit(solution)/shard_map/all_to_all | solution.py:37
  20.8 6.0 %gather_fusion = bf16[64,32,2,128]{3,2,1,0:T(2,128)(2,1)S(1)} fusion(bf16[512,32,2,128]{3,2,1,0:T(2,128)(2,1)} %param.12, s32[1024]{0:T(1024)S(1)} %pad_clamp_fusion.1), kind=kCustom, calls=%fused_computation | custom fusion | bytes 2097408 | tf_op jit(solution)/shard_map/jit(_take)/gather | solution.py:32
  29.8 13.7 %all-reduce = s32[1024]{0:T(1024)S(1)} all-reduce(s32[1024]{0:T(1024)S(1)} %dynamic-update-slice), channel_id=1, replica_groups=mesh['req'=32,'tp'=8] {'req'}, use_global_device_ids=true, to_apply=%add | all-reduce | flops 1024 | bytes 8192
  47.1 2.4 broadcast_select_fusion.2
  50.0 7.1 %all-to-all-start.1 = ((bf16[64,32,2,128]{3,2,1,0:T(2,128)(2,1)}), bf16[64,32,2,128]{3,2,1,0:T(2,128)(2,1)S(1)}, u32[]{:S(2)}, u32[]{:S(2)}) async-start(bf16[64,32,2,128]{3,2,1,0:T(2,128)(2,1)} %broadcast_select_fusion.2), calls=%async_computation.1 | async-start | bytes 2097152 | tf_op jit(solution)/shard_map/all_to_all | solution.py:36
  58.0 24.3 %all-to-all-done.1 = bf16[64,32,2,128]{3,2,1,0:T(2,128)(2,1)S(1)} async-done(((bf16[64,32,2,128]{3,2,1,0:T(2,128)(2,1)}), bf16[64,32,2,128]{3,2,1,0:T(2,128)(2,1)S(1)}, u32[]{:S(2)}, u32[]{:S(2)}) %all-to-all-start.1) | async-done | bytes 1048608 | tf_op jit(solution)/shard_map/all_to_all | solution.py:36
  82.3 25.9 %pad_maximum_fusion = bf16[576,32,2,128]{3,2,1,0:T(2,128)(2,1)} fusion(bf16[64,32,2,128]{3,2,1,0:T(2,128)(2,1)S(1)} %all-to-all-done.1, bf16[512,32,2,128]{3,2,1,0:T(2,128)(2,1)} %param.12), kind=kLoop, calls=%fused_computation.2 | loop fusion | flops 4718592 | bytes 18874368 | tf_op jit(solution)/shard_map/concatenate | solution.py:42
  108.2 30.0 %gather_fusion.1 = bf16[512,32,2,128]{3,2,1,0:T(2,128)(2,1)} fusion(bf16[576,32,2,128]{3,2,1,0:T(2,128)(2,1)} %pad_maximum_fusion, s32[1024]{0:T(1024)S(1)} %pad_clamp_fusion), kind=kCustom, calls=%fused_computation.1 | custom fusion | bytes 16779264 | tf_op jit(solution)/shard_map/jit(_take)/gather | solution.py:46
  138.2 7.9 %copy.25 = bf16[512,32,2,128]{3,1,0,2:T(8,128)(2,1)} copy(bf16[512,32,2,128]{3,2,1,0:T(2,128)(2,1)} %gather_fusion.1) | data formatting | bytes 16777216 | tf_op jit(solution)/shard_map/jit(_take)/gather | solution.py:46
  146.1 5.3 %broadcast_select_fusion = bf16[32,512,2,1,128]{4,1,0,3,2:T(8,128)(2,1)S(1)} fusion(bf16[32,512,2,1,128]{4,1,0,3,2:T(8,128)(2,1)} %bitcast.129, pred[32,512]{1,0:T(8,128)(4,1)S(1)} %broadcast_in_dim.174), kind=kLoop, calls=%fused_computation.3 | loop fusion | flops 4194304 | bytes 16793600 | tf_op jit(solution)/shard_map/jit(_take)/select_n | solution.py:46
  151.5 1.6 bitcast_reduce_fusion
  155.8 5.8 %fusion.30 = f32[128,4096]{0,1:S(1)} fusion(bf16[1024,4096]{0,1:T(8,128)(2,1)} %bitcast.132, bf16[16,8,8,128]{3,2,1,0:T(8,128)(2,1)S(1)} %bitcast.137), kind=kOutput, calls=%fused_computation.85 | convolution fusion | flops 1073741824 | bytes 10747904
  163.3 45.8 %all-gather.8.cloned.1.call-done = f32[4096,64]{0,1:T(8,128)} async-done(((f32[128,64]{0,1:T(8,128)}), f32[4096,64]{0,1:T(8,128)}) %all-gather.8.cloned.1.call-update) | async-done | bytes 1048592 | tf_op jit(solution)/shard_map/all_gather | solution.py:143
  209.5 59.6 %all-gather.4.cloned.1.call-done = bf16[4096,1024]{1,0:T(8,128)(2,1)} async-done(((bf16[128,1024]{1,0:T(8,128)(2,1)}), bf16[4096,1024]{1,0:T(8,128)(2,1)}) %all-gather.4.cloned.1.call-update) | async-done | bytes 8388624 | tf_op jit(solution)/shard_map/all_gather | solution.py:117
  269.0 7.7 %fusion.33 = f32[4096,256]{1,0:T(8,128)} fusion(bf16[4096,1024]{1,0:T(8,128)(2,1)} %all-gather.4.cloned.1.call-done, bf16[1024,256]{1,0:T(8,128)(2,1)S(1)} %copy-done), kind=kOutput, calls=%fused_computation.88 | convolution fusion | flops 2147483648 | bytes 13107200 | tf_op jit(solution)/shard_map/dot_general | solution.py:126
  278.3 6.9 %copy.26 = bf16[2,64,8192]{1,0,2:T(2,128)(2,1)} copy(bf16[2,64,8192]{2,1,0:T(8,128)(2,1)S(1)} %copy-done.1) | data formatting | bytes 4194304 | tf_op args[8]
  285.2 9.8 %reshape.331 = bf16[32,2,16384]{2,1,0:T(2,128)(2,1)} reshape(bf16[8192,2,64]{2,1,0:T(2,128)(2,1)} %bitcast.131) | data formatting | bytes 4194304
  295.0 5.5 %all-to-all-start.2 = ((bf16[32,2,16384]{2,1,0:T(2,128)(2,1)}), bf16[32,2,16384]{2,1,0:T(2,128)(2,1)S(1)}, u32[]{:S(2)}, u32[]{:S(2)}) async-start(bf16[32,2,16384]{2,1,0:T(2,128)(2,1)} %reshape.331), calls=%async_computation.4 | async-start | bytes 4194304 | tf_op jit(solution)/shard_map/all_to_all | solution.py:145
  300.6 28.2 %all-to-all-done.2 = bf16[32,2,16384]{2,1,0:T(2,128)(2,1)S(1)} async-done(((bf16[32,2,16384]{2,1,0:T(2,128)(2,1)}), bf16[32,2,16384]{2,1,0:T(2,128)(2,1)S(1)}, u32[]{:S(2)}, u32[]{:S(2)}) %all-to-all-start.2) | async-done | bytes 2097184 | tf_op jit(solution)/shard_map/all_to_all | solution.py:145
  328.9 4.0 %reshape.332 = bf16[8192,2,64]{2,1,0:T(2,128)(2,1)} reshape(bf16[32,2,16384]{2,1,0:T(2,128)(2,1)S(1)} %all-to-all-done.2) | data formatting | bytes 4194304
  332.9 9.3 %copy.34 = bf16[2,64,32,256]{3,1,0,2:T(8,128)(2,1)S(1)} copy(bf16[2,64,32,256]{1,0,3,2:T(2,128)(2,1)} %bitcast.130) | data formatting | bytes 4194304 | tf_op jit(solution)/shard_map/all_to_all | solution.py:145
  343.1 2.2 broadcast_multiply_fusion
  345.3 20.7 %reduce-scatter.3.cloned.1.call-done = f32[512,256]{1,0:T(8,128)} async-done(((f32[4096,256]{1,0:T(8,128)}), f32[512,256]{1,0:T(8,128)}) %reduce-scatter.3.cloned.1.call-update) | async-done | bytes 524304 | tf_op jit(solution)/shard_map/reduce_scatter | solution.py:125
  366.0 4.3 %fusion.5 = bf16[512,256]{1,0:T(8,128)(2,1)} fusion(f32[512,256]{1,0:T(8,128)} %reduce-scatter.3.cloned.1.call-done, bf16[512,4096]{0,1:T(8,128)(2,1)} %bitcast.134, bf16[4096,256]{1,0:T(8,128)(2,1)S(1)} %bitcast.135), kind=kOutput, calls=%fused_computation.21 | convolution fusion | flops 1074003968 | bytes 7077888 | tf_op jit(solution)/shard_map/dot_general | solution.py:156
  (66 shorter events, 20.1 us)
Async XLA Ops:
  6.5 262.5 %copy-start = (bf16[1024,256]{1,0:T(8,128)(2,1)S(1)}, bf16[1024,256]{1,0:T(8,128)(2,1)}, u32[]{:S(2)}) copy-start(bf16[1024,256]{1,0:T(8,128)(2,1)} %param.19) | copy-start | bytes 1572868
  6.5 149.2 %all-gather.6.cloned.1.call-start = ((), (), s32[]{:S(2)}) async-start(), calls=%async_computation.7 | async-start | bytes 8650752 | tf_op jit(solution)/shard_map/all_gather | solution.py:131
  11.2 38.8 %all-to-all-start = ((s32[32,2,1]{1,2,0:T(1,128)}), s32[32,2,1]{1,2,0:T(1,128)S(1)}, u32[]{:S(2)}, u32[]{:S(2)}) async-start(s32[32,2,1]{1,2,0:T(1,128)} %bitcast.3), calls=%async_computation | async-start | bytes 32768 | tf_op jit(solution)/shard_map/all_to_all | solution.py:37
  50.0 32.3 %all-to-all-start.1 = ((bf16[64,32,2,128]{3,2,1,0:T(2,128)(2,1)}), bf16[64,32,2,128]{3,2,1,0:T(2,128)(2,1)S(1)}, u32[]{:S(2)}, u32[]{:S(2)}) async-start(bf16[64,32,2,128]{3,2,1,0:T(2,128)(2,1)} %broadcast_select_fusion.2), calls=%async_computation.1 | async-start | bytes 2097152 | tf_op jit(solution)/shard_map/all_to_all | solution.py:36
  57.2 152.0 %all-gather.8.cloned.1.call-start = ((), (), s32[]{:S(2)}) async-start(), calls=%async_computation.8 | async-start | bytes 1081344 | tf_op jit(solution)/shard_map/all_gather | solution.py:143
  162.5 106.6 %all-gather.4.cloned.1.call-start = ((), (), s32[]{:S(2)}) async-start(), calls=%async_computation.5 | async-start | bytes 8650752 | tf_op jit(solution)/shard_map/all_gather | solution.py:117
  163.3 178.9 %reduce-scatter.5.cloned.1.call-start = ((), (), s32[]{:S(2)}) async-start(), calls=%async_computation.9 | async-start | bytes 1179648 | tf_op jit(solution)/shard_map/reduce_scatter | solution.py:144
  209.2 156.8 %reduce-scatter.3.cloned.1.call-start = ((), (), s32[]{:S(2)}) async-start(), calls=%async_computation.6 | async-start | bytes 4718592 | tf_op jit(solution)/shard_map/reduce_scatter | solution.py:125
  276.7 1.6 copy-start.1
  295.0 33.8 %all-to-all-start.2 = ((bf16[32,2,16384]{2,1,0:T(2,128)(2,1)}), bf16[32,2,16384]{2,1,0:T(2,128)(2,1)S(1)}, u32[]{:S(2)}, u32[]{:S(2)}) async-start(bf16[32,2,16384]{2,1,0:T(2,128)(2,1)} %reshape.331), calls=%async_computation.4 | async-start | bytes 4194304 | tf_op jit(solution)/shard_map/all_to_all | solution.py:145
Sparse Core Ops, SparseCore 0:
  9.9 72.5 all-gather.5
  162.6 46.5 all-gather.7
  211.7 57.2 all-gather.3
  271.4 33.2 reduce-scatter.4
  307.1 58.8 reduce-scatter.2
where the time goes:
time: 378 us; the launch traced here: 377 us
  waiting for transfers between devices  179 us (47%)
  local copies, waits for them, and re-layouts  82.3 us (22%)
  other arithmetic  43.6 us (12%)
  matrix products  22.1 us (6%)
  starting transfers between devices  21.6 us (6%)
  between operations  14.1 us (4%)
  blocking collectives  13.7 us (4%)
    all_gather x1, waiting for transfers between devices, on_device(): lax.all_gather(attention_mixed_output, 'req', axis=0, tiled=True)  59.6 us
    all_gather x1, waiting for transfers between devices, on_device(): lax.all_gather(adapter_partial, 'req', axis=0, tiled=True)  45.8 us
    gather x2, local copies, waits for them, and re-layouts, relocate(): return jnp.take(candidates, slot_source, axis=0)  37.9 us
    all_to_all x1, waiting for transfers between devices, on_device(): lax.all_to_all(adapter_up_factor, 'req', split_axis=2, concat_axis=0, til...  28.2 us
    unnamed x12, local copies, waits for them, and re-layouts  26.2 us
    concatenate x1, other arithmetic, relocate(): candidates = jnp.concatenate([key_value_pages, inbox_pages], axis=0)  25.9 us
    all_to_all x1, waiting for transfers between devices, relocate(): lax.all_to_all(outbox, 'req', split_axis=0, concat_axis=0, tiled=True)  24.3 us
    reduce_scatter x1, waiting for transfers between devices, on_device(): lax.psum_scatter(jnp.dot(everyone, output_projection_weight, preferred_el...  20.7 us
  transfers between devices with their start and end apart: 8, of which 5 were waited for; matrix products, arithmetic and copies ran while one was open for 36% of the time, Pallas kernels for 0%

commit v1 on v0

v1 whole, which is shorter than its diff:
```python
import functools
import math

import jax
import jax.numpy as jnp
from jax import lax
from jax.experimental import pallas as pl
from jax.experimental.pallas import tpu as pltpu
from jax.sharding import PartitionSpec as P

QUERY_HEADS = 64
KEY_VALUE_HEADS = 8
GROUP = QUERY_HEADS // KEY_VALUE_HEADS
HEAD_WIDTH = 128
STEP_COUNT = 4
PAGE_LENGTH = 32
PAGE_ROWS = 2 * PAGE_LENGTH
MAXP = 16
CAP = 2
VMEM_BYTES = 60 * 1024 * 1024


def pick_kernel(source, pages, outbox, sem):
    count = outbox.shape[0] // PAGE_ROWS

    def copy(k):
        start = pl.multiple_of(source[k] * PAGE_ROWS, PAGE_ROWS)
        put = pl.multiple_of(k * PAGE_ROWS, PAGE_ROWS)
        return pltpu.make_async_copy(
            pages.at[pl.ds(start, PAGE_ROWS), :], outbox.at[pl.ds(put, PAGE_ROWS), :], sem
        )

    for k in range(count):
        copy(k).start()
    pltpu.make_async_copy(pages.at[pl.ds(0, count * PAGE_ROWS), :], outbox, sem).wait()


def pick(out_source, pages):
    count = out_source.shape[0]
    return pl.pallas_call(
        pick_kernel,
        out_shape=jax.ShapeDtypeStruct((count * PAGE_ROWS, HEAD_WIDTH), pages.dtype),
        grid_spec=pltpu.PrefetchScalarGridSpec(
            num_scalar_prefetch=1,
            grid=(1,),
            in_specs=[pl.BlockSpec(memory_space=pl.ANY)],
            out_specs=pl.BlockSpec((count * PAGE_ROWS, HEAD_WIDTH), lambda i, s: (0, 0)),
            scratch_shapes=[pltpu.SemaphoreType.DMA],
        ),
        name="pick",
    )(out_source, pages)


def exchange_kernel(
    n, outbox, labels, up, inbox, inlab, upin, sent, got, lab_sent, lab_got, up_sent, up_got, own_sem
):
    me = lax.axis_index("req")
    lane = lax.axis_index("tp")
    block = CAP * PAGE_ROWS
    rows, columns = upin.shape[1], upin.shape[2]

    barrier = pltpu.get_barrier_semaphore()

    def greet(d, carry):
        pl.semaphore_signal(barrier, inc=1, device_id={"req": lax.rem(me + d, n)})
        return carry

    lax.fori_loop(1, n, greet, 0)
    pl.semaphore_wait(barrier, n - 1)

    def up_part(peer):
        return up.at[
            pl.ds(pl.multiple_of(lane * rows, rows), rows),
            pl.ds(pl.multiple_of(peer * columns, columns), columns),
        ]

    def copies(d):
        peer = lax.rem(me + d, n)
        to = {"req": peer}
        return (
            pltpu.make_async_remote_copy(
                labels.at[peer], inlab.at[me], lab_sent.at[d - 1], lab_got.at[d - 1], device_id=to
            ),
            pltpu.make_async_remote_copy(
                outbox.at[pl.ds(pl.multiple_of(peer * block, block), block), :],
                inbox.at[pl.ds(pl.multiple_of(me * block, block), block), :],
                sent.at[d - 1],
                got.at[d - 1],
                device_id=to,
            ),
            pltpu.make_async_remote_copy(
                up_part(peer), upin.at[me], up_sent.at[d - 1], up_got.at[d - 1], device_id=to
            ),
        )

    own = pltpu.make_async_copy(up_part(me), upin.at[me], own_sem)
    own.start()

    def begin(d, carry):
        for copy in copies(d):
            copy.start()
        return carry

    lax.fori_loop(1, n, begin, 0)

    def finish(d, carry):
        for copy in copies(d):
            copy.wait()
        return carry

    lax.fori_loop(1, n, finish, 0)
    own.wait()


def exchange(outbox, labels, up, n, tp_count):
    rows, columns = up.shape[0] // tp_count, up.shape[1] // n
    any_space = pl.BlockSpec(memory_space=pl.ANY)
    return pl.pallas_call(
        functools.partial(exchange_kernel, n),
        out_shape=(
            jax.ShapeDtypeStruct(outbox.shape, outbox.dtype),
            jax.ShapeDtypeStruct(labels.shape, labels.dtype),
            jax.ShapeDtypeStruct((n, rows, columns), up.dtype),
        ),
        in_specs=[any_space] * 3,
        out_specs=[any_space] * 3,
        scratch_shapes=[pltpu.SemaphoreType.DMA((n - 1,))] * 6 + [pltpu.SemaphoreType.DMA],
        compiler_params=pltpu.CompilerParams(collective_id=0, has_side_effects=True),
        name="exchange",
    )(outbox, labels, up)


def attend_kernel(table, lengths, queries, fresh, pages, inbox, out, cands, outf, sem):
    n_local, n_in = pages.shape[0], inbox.shape[0]
    requests = fresh.shape[0]
    load_local = pltpu.make_async_copy(pages, cands.at[pl.ds(0, n_local), :], sem.at[0])
    load_in = pltpu.make_async_copy(inbox, cands.at[pl.ds(n_local, n_in), :], sem.at[1])
    load_local.start()
    load_in.start()
    load_local.wait()
    load_in.wait()
    old = MAXP * PAGE_ROWS
    width = old + HEAD_WIDTH
    rows = GROUP * STEP_COUNT
    column = lax.broadcasted_iota(jnp.int32, (rows, width), 1)
    step = lax.rem(lax.broadcasted_iota(jnp.int32, (rows, width), 0), STEP_COUNT)
    is_key = lax.rem(column, 2) == 0
    new_index = (column - old) // 2
    keep_new = is_key & (column >= old) & (new_index <= step)
    position = jnp.where(is_key & (column < old), column // 2, 1 << 20)
    scale = 1.0 / math.sqrt(HEAD_WIDTH)
    filler = jnp.zeros((HEAD_WIDTH - fresh.shape[1], HEAD_WIDTH), fresh.dtype)

    def one(request, query):
        pieces = []
        for j in range(MAXP):
            start = pl.multiple_of(table[request * MAXP + j] * PAGE_ROWS, PAGE_ROWS)
            pieces.append(cands[pl.ds(start, PAGE_ROWS), :])
        pieces.append(fresh[request])
        pieces.append(filler)
        stored = jnp.concatenate(pieces, axis=0)
        scores = (
            lax.dot_general(
                query, stored, (((1,), (1,)), ((), ())), preferred_element_type=jnp.float32
            )
            * scale
        )
        keep = keep_new | (position < lengths[request])
        scores = jnp.where(keep, scores, -jnp.inf)
        top = jnp.max(scores, axis=1, keepdims=True)
        weights = jnp.exp(scores - top)
        probs = weights / jnp.sum(weights, axis=1, keepdims=True)
        probs = pltpu.roll(probs, 1, 1).astype(jnp.bfloat16)
        return jnp.dot(probs, stored, preferred_element_type=jnp.float32)

    def pair(index, carry):
        base = pl.multiple_of(index * 2 * STEP_COUNT, 2 * STEP_COUNT)
        block = queries[pl.ds(base, 2 * STEP_COUNT), :].astype(jnp.float32)
        mixed = []
        for k in range(2):
            part = block[k * STEP_COUNT : (k + 1) * STEP_COUNT]
            query = jnp.concatenate(
                [part[:, h * HEAD_WIDTH : (h + 1) * HEAD_WIDTH] for h in range(GROUP)], axis=0
            ).astype(jnp.bfloat16)
            mixed.append(one(index * 2 + k, query))
        for h in range(GROUP):
            both = jnp.concatenate(
                [m[h * STEP_COUNT : (h + 1) * STEP_COUNT] for m in mixed], axis=0
            )
            outf[pl.ds(base, 2 * STEP_COUNT), h * HEAD_WIDTH : (h + 1) * HEAD_WIDTH] = both
        return carry

    lax.fori_loop(0, requests // 2, pair, 0)
    out[...] = outf[...].astype(out.dtype)


def attend(table, lengths, queries, fresh, pages, inbox):
    tokens, width = queries.shape
    hbm = pl.BlockSpec(memory_space=pltpu.HBM)
    vmem = pl.BlockSpec(memory_space=pltpu.VMEM)
    smem = pl.BlockSpec(memory_space=pltpu.SMEM)
    return pl.pallas_call(
        attend_kernel,
        out_shape=jax.ShapeDtypeStruct((tokens, width), queries.dtype),
        in_specs=[smem, smem, vmem, vmem, hbm, hbm],
        out_specs=vmem,
        scratch_shapes=[
            pltpu.VMEM((pages.shape[0] + inbox.shape[0], HEAD_WIDTH), pages.dtype),
            pltpu.VMEM((tokens, width), jnp.float32),
            pltpu.SemaphoreType.DMA((2,)),
        ],
        compiler_params=pltpu.CompilerParams(vmem_limit_bytes=32 * 1024 * 1024),
        name="attend",
    )(table, lengths, queries, fresh, pages, inbox)


def on_device(
    queries,
    incoming_key_value,
    key_value_pages,
    page_request_home,
    lengths,
    request_adapter_index,
    adapter_storage_slot,
    adapter_down_factor,
    adapter_up_factor,
    output_projection_weight,
):
    n = lax.axis_size("req")
    tp_count = lax.axis_size("tp")
    me = lax.axis_index("req")
    lane = lax.axis_index("tp")
    per_dev = key_value_pages.shape[0]
    requests = lengths.shape[0]
    total = n * per_dev
    pages = key_value_pages.reshape(per_dev * PAGE_ROWS, HEAD_WIDTH)

    numbers = jnp.arange(per_dev, dtype=jnp.int32)
    peers = jnp.arange(n, dtype=jnp.int32)
    owner = page_request_home // per_dev
    match = (owner[:, None] == peers[None, :]) & (owner != me)[:, None]
    key = (numbers * total + page_request_home)[:, None]
    low_key = jnp.min(jnp.where(match, key, jnp.int32(2**30)), axis=0)
    high_key = jnp.max(jnp.where(match, key, -1), axis=0)
    keys = jnp.stack([low_key, high_key], axis=1)
    there = jnp.stack([high_key >= 0, high_key > low_key], axis=1)
    out_source = jnp.where(there, keys // total, 0).reshape(-1)
    out_label = jnp.where(there, keys % total, -1)

    slot_count = adapter_storage_slot.shape[0]
    slots = jnp.arange(slot_count, dtype=jnp.int32)
    own_slot = jnp.sum(
        jnp.where(
            request_adapter_index[:, None] == slots[None, :], adapter_storage_slot[None, :], 0
        ),
        axis=1,
    )
    labels = jnp.concatenate(
        [
            out_label,
            jnp.zeros((n, 64 - CAP), jnp.int32),
            jnp.broadcast_to(own_slot[None, :], (n, requests)),
            jnp.zeros((n, 64 - requests), jnp.int32),
        ],
        axis=1,
    ).reshape(n, 1, 128)

    outbox = pick(out_source, pages)
    up = adapter_up_factor.reshape(-1, adapter_up_factor.shape[2])
    inbox, inlab, upin = exchange(outbox, labels, up, n, tp_count)
    up_all = lax.all_gather(upin, "tp", axis=0, tiled=False)

    mine = (peers == me)[:, None]
    arrived = jnp.where(mine, -1, inlab[:, 0, :CAP]).reshape(-1)
    own_label = jnp.where(owner == me, page_request_home - me * per_dev, -1)
    in_label = jnp.where(arrived >= 0, arrived - me * per_dev, -1)
    candidate = jnp.concatenate([own_label, in_label], axis=0)
    candidate_numbers = jnp.arange(candidate.shape[0], dtype=jnp.int32)
    table = jnp.sum(
        jnp.where(candidate[:, None] == numbers[None, :], candidate_numbers[:, None], 0), axis=0
    )
    req_slot = jnp.where(mine, own_slot[None, :], inlab[:, 0, 64 : 64 + requests]).reshape(-1)
    token_slot = jnp.repeat(req_slot, STEP_COUNT)

    fresh = jnp.transpose(incoming_key_value, (1, 0, 2)).reshape(
        requests, 2 * STEP_COUNT, HEAD_WIDTH
    )
    fresh = jnp.pad(fresh, ((0, 0), (0, 8), (0, 0)))
    mixed = attend(table, lengths, queries, fresh, pages, inbox)

    everyone = lax.all_gather(mixed, "req", axis=0, tiled=True)
    own_adapters, _, rank = adapter_down_factor.shape
    down = jnp.transpose(adapter_down_factor, (1, 0, 2)).reshape(-1, own_adapters * rank)
    columns = output_projection_weight.shape[1]
    weights = jnp.concatenate([output_projection_weight, down], axis=1)
    product = jnp.dot(everyone, weights, preferred_element_type=jnp.float32)
    spot = jnp.arange(columns + own_adapters * rank, dtype=jnp.int32)
    spot_slot = jnp.where(spot < columns, -1, me * own_adapters + (spot - columns) // rank)
    keep = (spot_slot[None, :] < 0) | (spot_slot[None, :] == token_slot[:, None])
    partial = jnp.where(keep, product, 0.0).astype(jnp.bfloat16)
    reduced = lax.psum_scatter(partial, "tp", scatter_dimension=0, tiled=True)
    low = reduced[:, columns : columns + rank]
    for k in range(1, own_adapters):
        low = low + reduced[:, columns + k * rank : columns + (k + 1) * rank]
    low = lax.psum(low, "req")
    block_rows = reduced.shape[0]
    up_columns = jnp.transpose(up_all, (1, 0, 2, 3)).reshape(slot_count * rank, columns)
    block_slot = lax.dynamic_slice_in_dim(token_slot, lane * block_rows, block_rows)
    selector = (block_slot[:, None] == slots[None, :]).astype(jnp.bfloat16)
    expanded = (selector[:, :, None] * low[:, None, :]).reshape(block_rows, slot_count * rank)
    extra = jnp.dot(expanded, up_columns, preferred_element_type=jnp.float32)
    return (reduced[:, :columns].astype(jnp.float32) + extra).astype(jnp.bfloat16)


def solution(mesh):
    return jax.shard_map(
        on_device,
        mesh=mesh,
        in_specs=(
            P("req", "tp"),
            P(None, "req", "tp"),
            P("req", None, None, "tp"),
            P("req"),
            P("req"),
            P("req"),
            P(),
            P("req", "tp", None),
            P("req", None, None),
            P("tp", "req"),
        ),
        out_specs=P("tp", "req"),
        check_vma=False,
    )
```

time: 378 us -> 351 us (0.929)
  waiting for transfers between devices: 179 us -> 262 us
  local copies, waits for them, and re-layouts: 82.3 us -> 10.5 us
  Pallas kernels: 0 us -> 50.4 us
  other arithmetic: 43.6 us -> 4.56 us
  starting transfers between devices: 21.6 us -> 0.12 us
  blocking collectives: 13.7 us -> 0 us
  matrix products: 22.1 us -> 10.4 us
    psum x0 -> x1, waiting for transfers between devices: none -> 115 us  [on_device(): low = lax.psum(low, 'req')]
    all_to_all x3 -> x0, waiting for transfers between devices: 52.5 us -> none  [the longest x1 28.2 us: on_device(): lax.all_to_all(adapter_up_factor, 'req', split_axis=2, concat_axis=0, til...]
    pallas_call x0 -> x3, Pallas kernels: none -> 50.4 us  [the longest x1 27.4 us: exchange(): pl.pallas_call(functools.partial(exchange_kernel, n), out_shape=(jax.Shap...]
    gather x3 -> x0, local copies, waits for them, and re-layouts: 44 us -> none  [the longest x2 37.9 us: relocate(): return jnp.take(candidates, slot_source, axis=0)]
    concatenate x2, other arithmetic: 25.9 us -> 0.7 us  [the longest x1 0.69 us: on_device(): jnp.concatenate([out_label, jnp.zeros((n, 64 - CAP), jnp.int32), jnp.broa...]
    reduce_scatter x2 -> x1, waiting for transfers between devices: 20.7 us -> 42.4 us  [on_device(): reduced = lax.psum_scatter(partial, 'tp', scatter_dimension=0, tiled=True)]
    unnamed x12 -> x22, local copies, waits for them, and re-layouts: 26.2 us -> 4.64 us
    all_to_all x3 -> x0, starting transfers between devices: 21.2 us -> none  [the longest x1 8.58 us: relocate(): lax.all_to_all(labels, 'req', split_axis=0, concat_axis=0, tiled=True)]
  transfers between devices with their start and end apart: 8 -> 4, of which waited for: 5 -> 4; matrix products, arithmetic and copies ran while one was open for 36% -> 1% of each run, Pallas kernels for 0% -> 0%
where the time goes in v1:
time: 351 us
  waiting for transfers between devices  262 us (75%)
  Pallas kernels  50.4 us (14%)
  between operations  13.4 us (4%)
  local copies, waits for them, and re-layouts  10.5 us (3%)
  matrix products  10.4 us (3%)
  other arithmetic  4.56 us (1%)
    psum x1, waiting for transfers between devices, on_device(): low = lax.psum(low, 'req')  115 us
    all_gather x1, waiting for transfers between devices, on_device(): everyone = lax.all_gather(mixed, 'req', axis=0, tiled=True)  64.1 us
    reduce_scatter x1, waiting for transfers between devices, on_device(): reduced = lax.psum_scatter(partial, 'tp', scatter_dimension=0, tiled=True)  42.4 us
    all_gather x1, waiting for transfers between devices, on_device(): up_all = lax.all_gather(upin, 'tp', axis=0, tiled=False)  39.3 us
    pallas_call x1, Pallas kernels, exchange(): pl.pallas_call(functools.partial(exchange_kernel, n), out_shape=(jax.Shap...  27.4 us
    pallas_call x1, Pallas kernels, attend(): pl.pallas_call(attend_kernel, out_shape=jax.ShapeDtypeStruct((tokens, wid...  19.3 us
    dot_general x1, matrix products, on_device(): product = jnp.dot(everyone, weights, preferred_element_type=jnp.float32)  8.35 us
  transfers between devices with their start and end apart: 4, of which 4 were waited for; matrix products, arithmetic and copies ran while one was open for 1% of the time, Pallas kernels for 0%

profile of v1, /device:TPU:1, one launch (start us, length us, event | category | flops | bytes accessed | tf_op | source)
XLA Modules:
  0.0 351.1 jit_solution(8648723138891751874)
XLA Ops:
  6.5 0.7 subtract_select_fusion
  8.2 0.5 fusion.14.source
  8.7 3.6 %pick.1.outbox = bf16[4096,128]{1,0:T(8,128)(2,1)} custom-call(s32[64]{0:T(128)} %fusion.14.source, bf16[32768,128]{1,0:T(8,128)(2,1)} %bitcast.21), custom_call_target="tpu_custom_call" | custom-call | tf_op jit(solution)/shard_map/pick/pallas_call | solution.py:40
  12.3 0.2 select_reduce_fusion.3
  12.5 0.7 add_add_fusion
  13.2 27.4 %exchange.1 = (bf16[4096,128]{1,0:T(8,128)(2,1)}, s32[32,1,128]{2,1,0:T(1,128)}, bf16[32,16,256]{2,1,0:T(8,128)(2,1)}) custom-call(bf16[4096,128]{1,0:T(8,128)(2,1)} %pick.1.outbox, s32[32,1,128]{2,1,0:T(1,128)} %bitcast.29, bf16[128,8192]{1,0:T(8,128)(2,1)} %bitcast.24), custom_call_target="tpu_custom_call" | custom-call | tf_op jit(solution)/shard_map/exchange/pallas_call | solution.py:118
  40.7 0.8 slice_reduce_fusion
  41.8 0.2 select_reduce_fusion.table
  42.1 3.4 copy-done
  45.5 1.2 copy-done.1
  46.7 19.3 %attend.1 = bf16[128,1024]{1,0:T(8,128)(2,1)} custom-call(s32[512]{0:T(512)S(1)} %select_reduce_fusion.table, s32[32]{0:T(128)S(1)} %copy-done.3, bf16[128,1024]{1,0:T(8,128)(2,1)S(1)} %copy-done.2, bf16[32,16,128]{2,1,0:T(8,128)(2,1)S(1)} %pad.4.fresh, bf16[32768,128]{1,0:T(8,128)(2,1)S(1)} %bitcast.22, bf16[4096,128]{1,0:T(8,128)(2,1)S(1)} %copy-done.1), custom_call_target="tpu_custom_call" | custom-call | tf_op jit(solution)/shard_map/attend/pallas_call | solution.py:202
  66.6 0.2 broadcast_in_dim.139
  66.8 0.3 eq.96
  67.3 64.1 %all-gather.4.cloned.1.call-done = bf16[4096,1024]{1,0:T(8,128)(2,1)} async-done(((bf16[128,1024]{1,0:T(8,128)(2,1)}), bf16[4096,1024]{1,0:T(8,128)(2,1)}) %all-gather.4.cloned.1.call-update) | async-done | bytes 8388624 | tf_op jit(solution)/shard_map/all_gather | solution.py:291
  131.4 8.3 %select_convert_fusion = bf16[4096,384]{1,0:T(8,128)(2,1)} fusion(bf16[4096,1024]{1,0:T(8,128)(2,1)} %all-gather.4.cloned.1.call-done, s32[384]{0:T(512)S(1)} %fusion.9, s32[4096]{0:T(1024)S(1)} %eq.96, pred[384]{0:T(512)(128)(4,1)S(1)} %broadcast_compare_fusion.1, bf16[1024,128]{1,0:T(8,128)(2,1)S(1)} %copy.70, bf16[1024,256]{1,0:T(8,128)(2,1)S(1)} %copy-done.8), kind=kOutput, calls=%fused_computation | convolution fusion | flops 3229089792 | bytes 12339072 | tf_op jit(solution)/shard_map/dot_general | solution.py:296
  139.8 0.7 all-gather.6.cloned.1.call-update
  140.6 42.4 %reduce-scatter.2.cloned.1.call-done = bf16[512,384]{1,0:T(8,128)(2,1)} async-done(((bf16[4096,384]{1,0:T(8,128)(2,1)}), bf16[512,384]{1,0:T(8,128)(2,1)}) %reduce-scatter.2.cloned.1.call-update) | async-done | bytes 393232 | tf_op jit(solution)/shard_map/reduce_scatter | solution.py:301
  183.0 1.7 slice_add_fusion
  184.8 39.3 %all-gather.6.cloned.1.call-done = bf16[256,16,256]{2,1,0:T(8,128)(2,1)} async-done(((bf16[32,16,256]{2,1,0:T(8,128)(2,1)}), bf16[256,16,256]{2,1,0:T(8,128)(2,1)}) %all-gather.6.cloned.1.call-update) | async-done | bytes 2097168 | tf_op jit(solution)/shard_map/all_gather | solution.py:271
  224.1 1.9 copy.72
  226.0 115.3 %all-reduce.3.cloned.1.call-done = bf16[512,64]{1,0:T(8,128)(2,1)} async-done(((bf16[512,64]{1,0:T(8,128)(2,1)}), bf16[512,64]{1,0:T(8,128)(2,1)}) %all-reduce.3.cloned.1.call-update) | async-done | bytes 65552 | tf_op jit(solution)/shard_map/psum | solution.py:305
  341.3 1.0 copy.71
  342.3 0.3 broadcast_multiply_fusion
  342.6 2.0 fusion
  (63 shorter events, 2.3 us)
Async XLA Ops:
  6.5 124.9 %all-gather.4.cloned.1.call-start = ((), (), s32[]{:S(2)}) async-start(), calls=%async_computation.1 | async-start | bytes 8650752 | tf_op jit(solution)/shard_map/all_gather | solution.py:291
  8.7 3.6 %copy-start.9 = (s32[64]{0:T(128)S(1)}, s32[64]{0:T(128)}, u32[]{:S(2)}) copy-start(s32[64]{0:T(128)} %param.16) | copy-start | bytes 772
  8.7 3.6 %copy-start.10 = (s32[32]{0:T(128)S(1)}, s32[32]{0:T(128)}, u32[]{:S(2)}) copy-start(s32[32]{0:T(128)} %param.15) | copy-start | bytes 388
  12.3 29.6 %copy-start.6 = (bf16[2,128,128]{2,1,0:T(8,128)(2,1)S(1)}, bf16[2,128,128]{2,1,0:T(8,128)(2,1)}, u32[]{:S(2)}) copy-start(bf16[2,128,128]{2,1,0:T(8,128)(2,1)} %param.11) | copy-start | bytes 196612
  12.3 29.7 %copy-start.2 = (bf16[128,1024]{1,0:T(8,128)(2,1)S(1)}, bf16[128,1024]{1,0:T(8,128)(2,1)}, u32[]{:S(2)}) copy-start(bf16[128,1024]{1,0:T(8,128)(2,1)} %queries.1) | copy-start | bytes 786436
  12.3 29.7 %copy-start.3 = (s32[32]{0:T(128)S(1)}, s32[32]{0:T(128)}, u32[]{:S(2)}) copy-start(s32[32]{0:T(128)} %lengths.1) | copy-start | bytes 388
  42.1 3.4 copy-start
  45.5 1.2 copy-start.1
  46.7 19.5 %copy-start.7 = (s32[32,1,128]{2,1,0:T(1,128)S(1)}, s32[32,1,128]{2,1,0:T(1,128)}, u32[]{:S(2)}) copy-start(s32[32,1,128]{2,1,0:T(1,128)} %get-tuple-element.8) | copy-start | bytes 49156
  46.7 20.4 %copy-start.4 = (bf16[2,1024,64]{1,2,0:T(8,128)(2,1)S(1)}, bf16[2,1024,64]{1,2,0:T(8,128)(2,1)}, u32[]{:S(2)}) copy-start(bf16[2,1024,64]{1,2,0:T(8,128)(2,1)} %param.17) | copy-start | bytes 786436
  46.7 84.7 %copy-start.8 = (bf16[1024,256]{1,0:T(8,128)(2,1)S(1)}, bf16[1024,256]{1,0:T(8,128)(2,1)}, u32[]{:S(2)}) copy-start(bf16[1024,256]{1,0:T(8,128)(2,1)} %param.19) | copy-start | bytes 1572868
  66.1 116.9 %reduce-scatter.2.cloned.1.call-start = ((), (), s32[]{:S(2)}) async-start(), calls=%async_computation.2 | async-start | bytes 3538944 | tf_op jit(solution)/shard_map/reduce_scatter | solution.py:301
  139.8 84.4 %all-gather.6.cloned.1.call-start = ((), (), s32[]{:S(2)}) async-start(), calls=%async_computation.4 | async-start | bytes 2359296 | tf_op jit(solution)/shard_map/all_gather | solution.py:271
  140.5 200.8 %all-reduce.3.cloned.1.call-start = ((), (), s32[]{:S(2)}) async-start(), calls=%async_computation.3 | async-start | bytes 262144 | tf_op jit(solution)/shard_map/psum | solution.py:305
  226.0 116.6 %copy-start.5 = (bf16[512,384]{1,0:T(8,128)(2,1)S(1)}, bf16[512,384]{1,0:T(8,128)(2,1)}, u32[]{:S(2)}) copy-start(bf16[512,384]{1,0:T(8,128)(2,1)} %reduce-scatter.2.cloned.1.call-done) | copy-start | bytes 1179652
Sparse Core Ops, SparseCore 0:
  66.2 65.1 all-gather.3
  139.9 43.1 reduce-scatter.1
  184.8 39.2 all-gather.5
  227.2 114.0 all-reduce.2

commit v2 on v1

--- a/solution.py
+++ b/solution.py
@@ -52,12 +52,14 @@
 
 
 def exchange_kernel(
-    n, outbox, labels, up, inbox, inlab, upin, sent, got, lab_sent, lab_got, up_sent, up_got, own_sem
+    n, planes, outbox, labels, up, inbox, inlab, upall,
+    sent, got, lab_sent, lab_got, up_sent, up_got, ring_sent, ring_got, own_sem,
 ):
     me = lax.axis_index("req")
     lane = lax.axis_index("tp")
     block = CAP * PAGE_ROWS
-    rows, columns = upin.shape[1], upin.shape[2]
+    rows, columns = upall.shape[2], upall.shape[3]
+    above, below = lax.rem(lane + 1, planes), lax.rem(lane + planes - 1, planes)
 
     barrier = pltpu.get_barrier_semaphore()
 
@@ -66,7 +68,9 @@
         return carry
 
     lax.fori_loop(1, n, greet, 0)
-    pl.semaphore_wait(barrier, n - 1)
+    pl.semaphore_signal(barrier, inc=1, device_id={"tp": above})
+    pl.semaphore_signal(barrier, inc=1, device_id={"tp": below})
+    pl.semaphore_wait(barrier, n + 1)
 
     def up_part(peer):
         return up.at[
@@ -74,57 +78,101 @@
             pl.ds(pl.multiple_of(peer * columns, columns), columns),
         ]
 
-    def copies(d):
+    def label_copy(d):
         peer = lax.rem(me + d, n)
-        to = {"req": peer}
-        return (
-            pltpu.make_async_remote_copy(
-                labels.at[peer], inlab.at[me], lab_sent.at[d - 1], lab_got.at[d - 1], device_id=to
-            ),
-            pltpu.make_async_remote_copy(
-                outbox.at[pl.ds(pl.multiple_of(peer * block, block), block), :],
-                inbox.at[pl.ds(pl.multiple_of(me * block, block), block), :],
-                sent.at[d - 1],
-                got.at[d - 1],
-                device_id=to,
-            ),
-            pltpu.make_async_remote_copy(
-                up_part(peer), upin.at[me], up_sent.at[d - 1], up_got.at[d - 1], device_id=to
-            ),
-        )
-
-    own = pltpu.make_async_copy(up_part(me), upin.at[me], own_sem)
+        return pltpu.make_async_remote_copy(
+            labels.at[peer],
+            inlab.at[me],
+            lab_sent.at[d - 1],
+            lab_got.at[d - 1],
+            device_id={"req": peer},
+        )
+
+    def up_copy(d):
+        peer = lax.rem(me + d, n)
+        return pltpu.make_async_remote_copy(
+            up_part(peer),
+            upall.at[me, lane],
+            up_sent.at[d - 1],
+            up_got.at[d - 1],
+            device_id={"req": peer},
+        )
+
+    def page_copy(d):
+        peer = lax.rem(me + d, n)
+        return pltpu.make_async_remote_copy(
+            outbox.at[pl.ds(pl.multiple_of(peer * block, block), block), :],
+            inbox.at[pl.ds(pl.multiple_of(me * block, block), block), :],
+            sent.at[d - 1],
+            got.at[d - 1],
+            device_id={"req": peer},
+        )
+
+    own = pltpu.make_async_copy(up_part(me), upall.at[me, lane], own_sem)
     own.start()
 
-    def begin(d, carry):
-        for copy in copies(d):
-            copy.start()
-        return carry
-
-    lax.fori_loop(1, n, begin, 0)
-
-    def finish(d, carry):
-        for copy in copies(d):
-            copy.wait()
-        return carry
-
-    lax.fori_loop(1, n, finish, 0)
+    def begin_up(d, carry):
+        up_copy(d).start()
+        return carry
+
+    def begin_pages(d, carry):
+        label_copy(d).start()
+        page_copy(d).start()
+        return carry
+
+    def finish_up(d, carry):
+        up_copy(d).wait()
+        return carry
+
+    def finish_pages(d, carry):
+        label_copy(d).wait()
+        page_copy(d).wait()
+        return carry
+
+    lax.fori_loop(1, n, begin_up, 0)
+    lax.fori_loop(1, n, begin_pages, 0)
+    lax.fori_loop(1, n, finish_up, 0)
     own.wait()
 
-
-def exchange(outbox, labels, up, n, tp_count):
-    rows, columns = up.shape[0] // tp_count, up.shape[1] // n
+    hops = planes // 2
+
+    def ring_copy(way, hop):
+        peer = above if way == 0 else below
+        origin = lax.rem(lane + planes + (hop if way == 1 else -hop), planes)
+        part = upall.at[:, origin]
+        if hop == hops - 1:
+            part = upall.at[pl.ds(way * (n // 2), n // 2), origin]
+        return pltpu.make_async_remote_copy(
+            part, part, ring_sent.at[way, hop], ring_got.at[way, hop], device_id={"tp": peer}
+        )
+
+    for hop in range(hops):
+        for way in range(2):
+            if hop:
+                ring_copy(way, hop - 1).wait_recv()
+            ring_copy(way, hop).start()
+    for way in range(2):
+        ring_copy(way, hops - 1).wait_recv()
+        for hop in range(hops):
+            ring_copy(way, hop).wait_send()
+    lax.fori_loop(1, n, finish_pages, 0)
+
+
+def exchange(outbox, labels, up, n, planes):
+    rows, columns = up.shape[0] // planes, up.shape[1] // n
     any_space = pl.BlockSpec(memory_space=pl.ANY)
     return pl.pallas_call(
-        functools.partial(exchange_kernel, n),
+        functools.partial(exchange_kernel, n, planes),
         out_shape=(
             jax.ShapeDtypeStruct(outbox.shape, outbox.dtype),
             jax.ShapeDtypeStruct(labels.shape, labels.dtype),
-            jax.ShapeDtypeStruct((n, rows, columns), up.dtype),
+            jax.ShapeDtypeStruct((n, planes, rows, columns), up.dtype),
         ),
         in_specs=[any_space] * 3,
         out_specs=[any_space] * 3,
-        scratch_shapes=[pltpu.SemaphoreType.DMA((n - 1,))] * 6 + [pltpu.SemaphoreType.DMA],
+        scratch_shapes=[pltpu.SemaphoreType.DMA((n - 1,))] * 6
+        + [pltpu.SemaphoreType.DMA((2, planes // 2))] * 2
+        + [pltpu.SemaphoreType.DMA],
         compiler_params=pltpu.CompilerParams(collective_id=0, has_side_effects=True),
         name="exchange",
     )(outbox, labels, up)
@@ -214,6 +262,430 @@
     )(table, lengths, queries, fresh, pages, inbox)
 
 
+def project_kernel(
+    mixed, weights, slots, up, out,
+    everyone, part, lowpart, sendbuf, recvbuf, lowsend, lowrecv, sumsend, sumrecv, lowfull, extra,
+    own_sem, s1_sent, s1_got, s2_sent, s2_got, relay_sent, relay_got, mate_sent, mate_got,
+    main_sent, main_got, low_sent, low_got, sum_sent, sum_got,
+):
+    me = lax.axis_index("req")
+    lane = lax.axis_index("tp")
+    planes = 8
+    core = lax.rem(me, 2)
+    cx, cy = me // 8, lax.rem(me // 2, 4)
+    first = cx * (1 - core) + cy * core
+    second = cy * (1 - core) + cx * core
+    chunk_rows = mixed.shape[0]
+    half = chunk_rows // 2
+    columns = out.shape[1]
+    above, below = lax.rem(lane + 1, planes), lax.rem(lane + planes - 1, planes)
+    mate = me + 1 - 2 * core
+
+    def spot(f, s, c):
+        f, s = lax.rem(f + 8, 4), lax.rem(s + 8, 4)
+        return f * (8 - 6 * c) + s * (2 + 6 * c) + c
+
+    def at(df, ds):
+        return spot(first + df, second + ds, core)
+
+    def mate_at(df, ds):
+        return spot(second + df, first + ds, 1 - core)
+
+    barrier = pltpu.get_barrier_semaphore()
+    for d in range(1, 4):
+        pl.semaphore_signal(barrier, inc=1, device_id={"req": at(d, 0)})
+        pl.semaphore_signal(barrier, inc=1, device_id={"req": at(0, d)})
+    pl.semaphore_signal(barrier, inc=1, device_id={"req": mate})
+    pl.semaphore_signal(barrier, inc=1, device_id={"tp": above})
+    pl.semaphore_signal(barrier, inc=1, device_id={"tp": below})
+    pl.semaphore_wait(barrier, 9)
+
+    def remote(src, dst, sent, got, **to):
+        return pltpu.make_async_remote_copy(src, dst, sent, got, device_id=to)
+
+    HALVES = (pl.ds(0, half), pl.ds(half, half))
+
+    def offset(k):
+        return k + (k // 2) * (5 - 2 * k)
+
+    def step_one(way, src_owner, src):
+        return remote(
+            src,
+            everyone.at[src_owner],
+            s1_sent.at[way],
+            s1_got.at[way],
+            req=at(1 if way == 0 else -1, 0),
+        )
+
+    def step_one_half(way):
+        owner = at(-1 if way == 0 else 1, 0)
+        ref = everyone.at[owner, HALVES[way]]
+        return remote(
+            ref, ref, s1_sent.at[2 + way], s1_got.at[2 + way], req=at(1 if way == 0 else -1, 0)
+        )
+
+    def step_two(k, way, src=None):
+        owner = at(offset(k), 0)
+        ref = everyone.at[owner]
+        return remote(
+            ref if src is None else src,
+            ref,
+            s2_sent.at[k, way],
+            s2_got.at[k, way],
+            req=at(0, 1 if way == 0 else -1),
+        )
+
+    def relay(k, way):
+        owner = at(offset(k), -1 if way == 0 else 1)
+        ref = everyone.at[owner, HALVES[way]]
+        return remote(
+            ref, ref, relay_sent.at[k, way], relay_got.at[k, way], req=at(0, 1 if way == 0 else -1)
+        )
+
+    DS = (0, -1, 1, 2)
+
+    def to_mate(k, j, src=None):
+        ref = everyone.at[at(offset(k), DS[j])]
+        return remote(
+            ref if src is None else src, ref, mate_sent.at[j, k], mate_got.at[j, k], req=mate
+        )
+
+    def arrived(ref, sem):
+        pltpu.make_async_copy(ref, ref, sem).wait()
+
+    def got_mate(k, j):
+        arrived(everyone.at[mate_at(offset(k), DS[j])], mate_got.at[j, k])
+
+    row = lax.broadcasted_iota(jnp.int32, (chunk_rows, HEAD_WIDTH), 0)
+    col = lax.broadcasted_iota(jnp.int32, (chunk_rows, HEAD_WIDTH), 1)
+    diagonal = row == col
+    narrow = lax.broadcasted_iota(jnp.int32, (half, HEAD_WIDTH), 1) < half
+    upper = col // half
+
+    def slot_column(r):
+        values = jnp.where(diagonal, slots[r].astype(jnp.float32), 0.0)
+        return jnp.sum(values, axis=1, keepdims=True).astype(jnp.int32)
+
+    def batch(owners):
+        rows = jnp.concatenate([everyone[r] for r in owners], axis=0)
+        product = jnp.dot(rows, weights[...], preferred_element_type=jnp.float32)
+        for i, r in enumerate(owners):
+            block = product[i * chunk_rows : (i + 1) * chunk_rows]
+            part[r] = block[:, :columns]
+            low = jnp.where(slot_column(r) == 2 * me + upper, block[:, columns:], 0.0)
+            low = low + pltpu.roll(low, half, 1)
+            lowpart[r] = jnp.where(narrow, low[:half], low[half:])
+
+    own = pltpu.make_async_copy(mixed, everyone.at[me], own_sem)
+    own.start()
+    step_one(0, me, mixed).start()
+    step_one(1, me, mixed).start()
+    step_two(0, 0, mixed).start()
+    step_two(0, 1, mixed).start()
+    to_mate(0, 0, mixed).start()
+
+    def pass_on(k):
+        step_two(k, 0).start()
+        step_two(k, 1).start()
+        to_mate(k, 0).start()
+
+    arrived(everyone.at[at(-1, 0)], s1_got.at[0])
+    step_one_half(0).start()
+    pass_on(2)
+    arrived(everyone.at[at(1, 0)], s1_got.at[1])
+    step_one_half(1).start()
+    pass_on(1)
+
+    def turn(k):
+        arrived(everyone.at[at(offset(k), -1)], s2_got.at[k, 0])
+        relay(k, 0).start()
+        to_mate(k, 1).start()
+        arrived(everyone.at[at(offset(k), 1)], s2_got.at[k, 1])
+        relay(k, 1).start()
+        to_mate(k, 2).start()
+
+    turn(0)
+    for way in range(2):
+        arrived(everyone.at[at(2, 0), HALVES[way]], s1_got.at[2 + way])
+    pass_on(3)
+    own.wait()
+
+    def batch_one(b, carry):
+        for k in range(2):
+            got_mate(2 * b + k, 0)
+        batch(
+            [at(offset(2 * b + k), 0) for k in range(2)]
+            + [mate_at(offset(2 * b + k), 0) for k in range(2)]
+        )
+        return carry
+
+    lax.fori_loop(0, 2, batch_one, 0)
+
+    def batch_two(k):
+        got_mate(k, 1)
+        got_mate(k, 2)
+        o = offset(k)
+        batch([at(o, -1), at(o, 1), mate_at(o, -1), mate_at(o, 1)])
+
+    def around(k, carry):
+        turn(k)
+        batch_two(k - 1)
+        return carry
+
+    lax.fori_loop(1, 4, around, 0)
+
+    def last(k):
+        for way in range(2):
+            arrived(everyone.at[at(offset(k), 2), HALVES[way]], relay_got.at[k, way])
+        to_mate(k, 3).start()
+
+    last(0)
+    last(1)
+    batch_two(3)
+    last(2)
+    last(3)
+
+    def batch_three(b, carry):
+        for k in range(2):
+            got_mate(2 * b + k, 3)
+        batch(
+            [at(offset(2 * b + k), 2) for k in range(2)]
+            + [mate_at(offset(2 * b + k), 2) for k in range(2)]
+        )
+        return carry
+
+    lax.fori_loop(0, 2, batch_three, 0)
+
+    hops = planes // 2
+    subs = planes // 2
+
+    def target(way, step):
+        return lax.rem(lane + planes + (step - hops if way == 0 else hops - step), planes)
+
+    def low_copy(way, step):
+        peer = below if way == 0 else above
+        src, dst = lowsend.at[way, step], lowrecv.at[way, step]
+        if step == 0:
+            part_of = pl.ds(way * (subs // 2), subs // 2)
+            src, dst = lowsend.at[way, step, part_of], lowrecv.at[way, step, part_of]
+        return remote(src, dst, low_sent.at[way, step], low_got.at[way, step], tp=peer)
+
+    def low_step(step):
+        for way in range(2):
+            if step:
+                low_copy(way, step - 1).wait_recv()
+            q = target(way, step)
+            for sub in range(subs):
+                fresh_half = sub // (subs // 2) == way
+                if step == 0 and not fresh_half:
+                    continue
+                value = lowpart[q * subs + sub]
+                if step > 1 or (step == 1 and fresh_half):
+                    value = value + lowrecv[way, step - 1, sub].astype(jnp.float32)
+                lowsend[way, step, sub] = value.astype(jnp.bfloat16)
+            low_copy(way, step).start()
+
+    def main_copy(way, step, sub):
+        peer = below if way == 0 else above
+        src, dst = sendbuf.at[way, step, sub], recvbuf.at[way, step, sub]
+        if step == 0:
+            side = pl.ds(way * (columns // 2), columns // 2)
+            src, dst = sendbuf.at[way, step, sub, :, side], recvbuf.at[way, step, sub, :, side]
+        return remote(src, dst, main_sent.at[way, step, sub], main_got.at[way, step, sub], tp=peer)
+
+    def main_step(step, sub):
+        for way in range(2):
+            q = target(way, step)
+            side = slice(way * (columns // 2), (way + 1) * (columns // 2))
+            if step == 0:
+                sendbuf[way, step, sub, :, side] = part[q * subs + sub, :, side].astype(jnp.bfloat16)
+            else:
+                main_copy(way, step - 1, sub).wait_recv()
+                value = part[q * subs + sub]
+                if step == 1:
+                    came = recvbuf[way, 0, sub, :, side].astype(jnp.float32)
+                    other = slice((1 - way) * (columns // 2), (2 - way) * (columns // 2))
+                    sendbuf[way, 1, sub, :, side] = (value[:, side] + came).astype(jnp.bfloat16)
+                    sendbuf[way, 1, sub, :, other] = value[:, other].astype(jnp.bfloat16)
+                else:
+                    came = recvbuf[way, step - 1, sub].astype(jnp.float32)
+                    sendbuf[way, step, sub] = (value + came).astype(jnp.bfloat16)
+            main_copy(way, step, sub).start()
+
+    def sum_mate():
+        return remote(
+            sumsend.at[0, 1 - core], sumrecv.at[0], sum_sent.at[0], sum_got.at[0], req=mate
+        )
+
+    def sum_axis(axis, d):
+        peer = at(d, 0) if axis == 0 else at(0, d)
+        i = 1 + 3 * axis + d - 1
+        return remote(
+            sumsend.at[1 + axis, 0], sumrecv.at[i], sum_sent.at[i], sum_got.at[i], req=peer
+        )
+
+    def sum_back():
+        return remote(
+            lowfull.at[core], lowfull.at[core], sum_sent.at[7], sum_got.at[7], req=mate
+        )
+
+    def low_end():
+        for way in range(2):
+            low_copy(way, hops - 1).wait_recv()
+        for sub in range(subs):
+            value = lowpart[lane * subs + sub]
+            for way in range(2):
+                value = value + lowrecv[way, hops - 1, sub].astype(jnp.float32)
+            sumsend[0, sub // 2, pl.ds(half * (sub % 2), half)] = value.astype(jnp.bfloat16)
+        sum_mate().start()
+
+    def sum_first():
+        sum_mate().wait_recv()
+        value = sumsend[0, core].astype(jnp.float32) + sumrecv[0].astype(jnp.float32)
+        sumsend[1, 0] = value.astype(jnp.bfloat16)
+        for d in range(1, 4):
+            sum_axis(0, d).start()
+
+    def gathered(axis):
+        value = sumsend[1 + axis, 0].astype(jnp.float32)
+        for d in range(1, 4):
+            sum_axis(axis, d).wait_recv()
+            value = value + sumrecv[1 + 3 * axis + d - 1].astype(jnp.float32)
+        return value.astype(jnp.bfloat16)
+
+    def sum_second():
+        sumsend[2, 0] = gathered(0)
+        for d in range(1, 4):
+            sum_axis(1, d).start()
+
+    def sum_third():
+        lowfull[core] = gathered(1)
+        sum_back().start()
+
+    def lora():
+        arrived(lowfull.at[1 - core], sum_got.at[7])
+        pieces, owners = [], []
+        for sub in range(subs):
+            packed = lowfull[sub // 2, pl.ds(half * (sub % 2), half)].astype(jnp.float32)
+            turned = pltpu.roll(packed, half, 1)
+            pieces.append(
+                jnp.concatenate(
+                    [jnp.where(narrow, packed, turned), jnp.where(narrow, turned, packed)], axis=0
+                )
+            )
+            owners.append(slot_column(lane * subs + sub))
+        low = jnp.concatenate(pieces, axis=0)
+        owner = jnp.concatenate(owners, axis=0)
+        side = lax.broadcasted_iota(jnp.int32, low.shape, 1) // half
+        group = 8
+        extra[...] = jnp.zeros(extra.shape, jnp.float32)
+
+        def add(g, carry):
+            wide = jnp.concatenate(
+                [
+                    jnp.where(owner == 2 * (g * group + m) + side, low, 0.0).astype(jnp.bfloat16)
+                    for m in range(group)
+                ],
+                axis=1,
+            )
+            rows = group * HEAD_WIDTH
+            block = up[pl.ds(pl.multiple_of(g * rows, rows), rows), :]
+            extra[...] += jnp.dot(wide, block, preferred_element_type=jnp.float32)
+            return carry
+
+        lax.fori_loop(0, up.shape[0] // (group * HEAD_WIDTH), add, 0)
+
+    low_step(0)
+    for sub in range(subs):
+        main_step(0, sub)
+    low_step(1)
+    main_step(1, 0)
+    main_step(1, 1)
+    low_step(2)
+    main_step(1, 2)
+    main_step(1, 3)
+    low_step(3)
+    main_step(2, 0)
+    main_step(2, 1)
+    low_end()
+    main_step(2, 2)
+    main_step(2, 3)
+    sum_first()
+    main_step(3, 0)
+    main_step(3, 1)
+    sum_second()
+    main_step(3, 2)
+    main_step(3, 3)
+    sum_third()
+    lora()
+    for sub in range(subs):
+        rows = pl.ds(sub * chunk_rows, chunk_rows)
+        value = part[lane * subs + sub] + extra[rows, :]
+        for way in range(2):
+            main_copy(way, hops - 1, sub).wait_recv()
+            value = value + recvbuf[way, hops - 1, sub].astype(jnp.float32)
+        out[rows, :] = value.astype(out.dtype)
+
+    for way in range(2):
+        step_one(way, me, mixed).wait_send()
+        step_one_half(way).wait_send()
+        for k in range(4):
+            step_two(k, way).wait_send()
+            relay(k, way).wait_send()
+        for step in range(hops):
+            low_copy(way, step).wait_send()
+            for sub in range(subs):
+                main_copy(way, step, sub).wait_send()
+    for k in range(4):
+        for j in range(4):
+            to_mate(k, j).wait_send()
+    sum_mate().wait_send()
+    for axis in range(2):
+        for d in range(1, 4):
+            sum_axis(axis, d).wait_send()
+    sum_back().wait_send()
+
+
+def project(mixed, weights, slots, up):
+    rows, depth = mixed.shape
+    n, columns, planes = slots.shape[0], up.shape[1], 8
+    vmem = pl.BlockSpec(memory_space=pltpu.VMEM)
+    dma = pltpu.SemaphoreType.DMA
+    bf16, f32 = jnp.bfloat16, jnp.float32
+    hops, subs, half = planes // 2, planes // 2, rows // 2
+    return pl.pallas_call(
+        project_kernel,
+        out_shape=jax.ShapeDtypeStruct((n * rows // planes, columns), bf16),
+        in_specs=[vmem] * 4,
+        out_specs=vmem,
+        scratch_shapes=[
+            pltpu.VMEM((n, rows, depth), bf16),
+            pltpu.VMEM((n, rows, columns), f32),
+            pltpu.VMEM((n, half, HEAD_WIDTH), f32),
+            pltpu.VMEM((2, hops, subs, rows, columns), bf16),
+            pltpu.VMEM((2, hops, subs, rows, columns), bf16),
+            pltpu.VMEM((2, hops, subs, half, HEAD_WIDTH), bf16),
+            pltpu.VMEM((2, hops, subs, half, HEAD_WIDTH), bf16),
+            pltpu.VMEM((3, 2, rows, HEAD_WIDTH), bf16),
+            pltpu.VMEM((7, rows, HEAD_WIDTH), bf16),
+            pltpu.VMEM((2, rows, HEAD_WIDTH), bf16),
+            pltpu.VMEM((n * rows // planes, columns), f32),
+            dma,
+            dma((4,)), dma((4,)),
+            dma((4, 2)), dma((4, 2)),
+            dma((4, 2)), dma((4, 2)),
+            dma((4, 4)), dma((4, 4)),
+            dma((2, hops, subs)), dma((2, hops, subs)),
+            dma((2, hops)), dma((2, hops)),
+            dma((8,)), dma((8,)),
+        ],
+        compiler_params=pltpu.CompilerParams(
+            collective_id=1, has_side_effects=True, vmem_limit_bytes=VMEM_BYTES
+        ),
+        name="project",
+    )(mixed, weights, slots, up)
+
+
 def on_device(
     queries,
     incoming_key_value,
@@ -229,7 +701,6 @@
     n = lax.axis_size("req")
     tp_count = lax.axis_size("tp")
     me = lax.axis_index("req")
-    lane = lax.axis_index("tp")
     per_dev = key_value_pages.shape[0]
     requests = lengths.shape[0]
     total = n * per_dev
@@ -267,8 +738,7 @@
 
     outbox = pick(out_source, pages)
     up = adapter_up_factor.reshape(-1, adapter_up_factor.shape[2])
-    inbox, inlab, upin = exchange(outbox, labels, up, n, tp_count)
-    up_all = lax.all_gather(upin, "tp", axis=0, tiled=False)
+    inbox, inlab, upall = exchange(outbox, labels, up, n, tp_count)
 
     mine = (peers == me)[:, None]
     arrived = jnp.where(mine, -1, inlab[:, 0, :CAP]).reshape(-1)
@@ -288,28 +758,15 @@
     fresh = jnp.pad(fresh, ((0, 0), (0, 8), (0, 0)))
     mixed = attend(table, lengths, queries, fresh, pages, inbox)
 
-    everyone = lax.all_gather(mixed, "req", axis=0, tiled=True)
     own_adapters, _, rank = adapter_down_factor.shape
     down = jnp.transpose(adapter_down_factor, (1, 0, 2)).reshape(-1, own_adapters * rank)
-    columns = output_projection_weight.shape[1]
     weights = jnp.concatenate([output_projection_weight, down], axis=1)
-    product = jnp.dot(everyone, weights, preferred_element_type=jnp.float32)
-    spot = jnp.arange(columns + own_adapters * rank, dtype=jnp.int32)
-    spot_slot = jnp.where(spot < columns, -1, me * own_adapters + (spot - columns) // rank)
-    keep = (spot_slot[None, :] < 0) | (spot_slot[None, :] == token_slot[:, None])
-    partial = jnp.where(keep, product, 0.0).astype(jnp.bfloat16)
-    reduced = lax.psum_scatter(partial, "tp", scatter_dimension=0, tiled=True)
-    low = reduced[:, columns : columns + rank]
-    for k in range(1, own_adapters):
-        low = low + reduced[:, columns + k * rank : columns + (k + 1) * rank]
-    low = lax.psum(low, "req")
-    block_rows = reduced.shape[0]
-    up_columns = jnp.transpose(up_all, (1, 0, 2, 3)).reshape(slot_count * rank, columns)
-    block_slot = lax.dynamic_slice_in_dim(token_slot, lane * block_rows, block_rows)
-    selector = (block_slot[:, None] == slots[None, :]).astype(jnp.bfloat16)
-    expanded = (selector[:, :, None] * low[:, None, :]).reshape(block_rows, slot_count * rank)
-    extra = jnp.dot(expanded, up_columns, preferred_element_type=jnp.float32)
-    return (reduced[:, :columns].astype(jnp.float32) + extra).astype(jnp.bfloat16)
+    return project(
+        mixed,
+        weights,
+        token_slot.reshape(n, 1, requests * STEP_COUNT),
+        upall.reshape(slot_count * rank, output_projection_weight.shape[1]),
+    )
 
 
 def solution(mesh):

time: 351 us -> 156 us (0.44)
  waiting for transfers between devices: 262 us -> 0 us
  Pallas kernels: 50.4 us -> 143 us
  between operations: 13.4 us -> 0.17 us
  matrix products: 10.4 us -> 0 us
    psum x1 -> x0, waiting for transfers between devices: 115 us -> none  [on_device(): low = lax.psum(low, 'req')]
    all_gather x2 -> x0, waiting for transfers between devices: 103 us -> none  [the longest x1 64.1 us: on_device(): everyone = lax.all_gather(mixed, 'req', axis=0, tiled=True)]
    pallas_call x1 -> x2, Pallas kernels: 27.4 us -> 120 us  [the longest x1 72.2 us: project(): pl.pallas_call(project_kernel, out_shape=jax.ShapeDtypeStruct((n * rows /...]
    reduce_scatter x1 -> x0, waiting for transfers between devices: 42.4 us -> none  [on_device(): reduced = lax.psum_scatter(partial, 'tp', scatter_dimension=0, tiled=True)]
    dot_general x2 -> x0, matrix products: 10.4 us -> none  [the longest x1 8.35 us: on_device(): product = jnp.dot(everyone, weights, preferred_element_type=jnp.float32)]
  transfers between devices with their start and end apart: 4 -> 0, of which waited for: 4 -> 0; matrix products, arithmetic and copies ran while one was open for 1% -> 0% of each run, Pallas kernels for 0% -> 0%
where the time goes in v2:
time: 156 us
  Pallas kernels  143 us (92%)
  local copies, waits for them, and re-layouts  9.82 us (6%)
  other arithmetic  3.55 us (2%)
    pallas_call x1, Pallas kernels, project(): pl.pallas_call(project_kernel, out_shape=jax.ShapeDtypeStruct((n * rows /...  72.2 us
    pallas_call x1, Pallas kernels, exchange(): pl.pallas_call(functools.partial(exchange_kernel, n, planes), out_shape=(...  48.1 us
    pallas_call x1, Pallas kernels, attend(): pl.pallas_call(attend_kernel, out_shape=jax.ShapeDtypeStruct((tokens, wid...  18.7 us
    unnamed x23, local copies, waits for them, and re-layouts  7 us
    pallas_call x1, Pallas kernels, pick(): pl.pallas_call(pick_kernel, out_shape=jax.ShapeDtypeStruct((count * PAGE_...  3.82 us

profile of v2, /device:TPU:1, one launch (start us, length us, event | category | flops | bytes accessed | tf_op | source)
XLA Modules:
  0.0 156.3 jit_solution(9601481925938862496)
XLA Ops:
  0.0 0.7 subtract_select_fusion
  0.7 0.1 select_reduce_fusion.2
  0.8 0.1 copy.56
  1.1 0.1 copy.55
  1.2 0.1 stack.15
  1.3 0.1 stack.17
  1.4 0.5 fusion.5.source
  1.9 3.8 %pick.1.outbox = bf16[4096,128]{1,0:T(8,128)(2,1)} custom-call(s32[64]{0:T(128)} %fusion.5.source, bf16[32768,128]{1,0:T(8,128)(2,1)} %bitcast.20), custom_call_target="tpu_custom_call" | custom-call | tf_op jit(solution)/shard_map/pick/pallas_call | solution.py:40
  5.8 0.2 select_reduce_fusion.3
  6.2 0.7 add_add_fusion
  6.9 48.1 %exchange.1 = (bf16[4096,128]{1,0:T(8,128)(2,1)}, s32[32,1,128]{2,1,0:T(1,128)}, bf16[32,8,16,256]{3,2,1,0:T(8,128)(2,1)}) custom-call(bf16[4096,128]{1,0:T(8,128)(2,1)} %pick.1.outbox, s32[32,1,128]{2,1,0:T(1,128)} %bitcast.27, bf16[128,8192]{1,0:T(8,128)(2,1)} %bitcast.22), custom_call_target="tpu_custom_call" | custom-call | tf_op jit(solution)/shard_map/exchange/pallas_call | solution.py:164
  55.0 0.8 slice_reduce_fusion
  55.7 0.1 squeeze.6
  55.9 0.1 broadcast_in_dim.113
  56.1 0.2 select_reduce_fusion.table
  56.4 3.4 %copy-done = bf16[512,32,2,128]{3,2,1,0:T(2,128)(2,1)S(1)} copy-done((bf16[512,32,2,128]{3,2,1,0:T(2,128)(2,1)S(1)}, bf16[512,32,2,128]{3,2,1,0:T(2,128)(2,1)}, u32[]{:S(2)}) %copy-start) | copy-done | bytes 8388632
  59.8 1.2 copy-done.2
  61.0 18.7 %attend.1.mixed = bf16[128,1024]{1,0:T(8,128)(2,1)S(1)} custom-call(s32[512]{0:T(512)S(1)} %select_reduce_fusion.table, s32[32]{0:T(128)S(1)} %copy-done.4, bf16[128,1024]{1,0:T(8,128)(2,1)S(1)} %copy-done.3, bf16[32,16,128]{2,1,0:T(8,128)(2,1)S(1)} %pad.4.fresh, bf16[32768,128]{1,0:T(8,128)(2,1)S(1)} %bitcast.21, bf16[4096,128]{1,0:T(8,128)(2,1)S(1)} %copy-done.2), custom_call_target="tpu_custom_call" | custom-call | tf_op jit(solution)/shard_map/attend/pallas_call | solution.py:250
  79.7 0.7 copy-done.1
  80.6 0.7 copy.66.slots
  81.2 0.2 copy.63
  81.4 1.0 pad_maximum_fusion.weights
  82.4 72.2 %project.1 = bf16[512,256]{1,0:T(8,128)(2,1)} custom-call(bf16[128,1024]{1,0:T(8,128)(2,1)} %copy-done.1, bf16[1024,384]{1,0:T(8,128)(2,1)} %pad_maximum_fusion.weights, s32[32,1,128]{2,1,0:T(1,128)} %copy.66.slots, bf16[4096,256]{1,0:T(8,128)(2,1)} %bitcast.23), custom_call_target="tpu_custom_call" | custom-call | tf_op jit(solution)/shard_map/project/pallas_call | solution.py:656
  154.6 1.7 %copy.68 = bf16[512,256]{1,0:T(8,128)(2,1)} copy(bf16[512,256]{1,0:T(8,128)(2,1)} %project.1) | data formatting | bytes 524288
  (40 shorter events, 0.8 us)
Async XLA Ops:
  1.9 3.9 %copy-start.9 = (s32[64]{0:T(128)S(1)}, s32[64]{0:T(128)}, u32[]{:S(2)}) copy-start(s32[64]{0:T(128)} %param.16) | copy-start | bytes 772
  1.9 3.9 %copy-start.10 = (s32[32]{0:T(128)S(1)}, s32[32]{0:T(128)}, u32[]{:S(2)}) copy-start(s32[32]{0:T(128)} %param.15) | copy-start | bytes 388
  6.9 49.4 %copy-start.7 = (bf16[2,128,128]{2,1,0:T(8,128)(2,1)S(1)}, bf16[2,128,128]{2,1,0:T(8,128)(2,1)}, u32[]{:S(2)}) copy-start(bf16[2,128,128]{2,1,0:T(8,128)(2,1)} %param.11) | copy-start | bytes 196612
  6.9 49.5 %copy-start.3 = (bf16[128,1024]{1,0:T(8,128)(2,1)S(1)}, bf16[128,1024]{1,0:T(8,128)(2,1)}, u32[]{:S(2)}) copy-start(bf16[128,1024]{1,0:T(8,128)(2,1)} %queries.1) | copy-start | bytes 786436
  6.9 49.5 %copy-start.4 = (s32[32]{0:T(128)S(1)}, s32[32]{0:T(128)}, u32[]{:S(2)}) copy-start(s32[32]{0:T(128)} %lengths.1) | copy-start | bytes 388
  56.4 3.4 %copy-start = (bf16[512,32,2,128]{3,2,1,0:T(2,128)(2,1)S(1)}, bf16[512,32,2,128]{3,2,1,0:T(2,128)(2,1)}, u32[]{:S(2)}) copy-start(bf16[512,32,2,128]{3,2,1,0:T(2,128)(2,1)} %param.12) | copy-start | bytes 25165828
  59.8 1.2 copy-start.2
  61.0 19.4 %copy-start.8 = (s32[32,1,128]{2,1,0:T(1,128)S(1)}, s32[32,1,128]{2,1,0:T(1,128)}, u32[]{:S(2)}) copy-start(s32[32,1,128]{2,1,0:T(1,128)} %get-tuple-element.8) | copy-start | bytes 49156
  61.0 20.2 %copy-start.6 = (bf16[2,1024,64]{1,2,0:T(8,128)(2,1)S(1)}, bf16[2,1024,64]{1,2,0:T(8,128)(2,1)}, u32[]{:S(2)}) copy-start(bf16[2,1024,64]{1,2,0:T(8,128)(2,1)} %param.17) | copy-start | bytes 786436
  61.0 20.4 %copy-start.5 = (bf16[1024,256]{1,0:T(8,128)(2,1)S(1)}, bf16[1024,256]{1,0:T(8,128)(2,1)}, u32[]{:S(2)}) copy-start(bf16[1024,256]{1,0:T(8,128)(2,1)} %param.19) | copy-start | bytes 1572868
  79.7 0.7 copy-start.1

commit v3 on v1

v3 whole, which is shorter than its diff:
```python
import functools
import math

import jax
import jax.numpy as jnp
from jax import lax
from jax.experimental import pallas as pl
from jax.experimental.pallas import tpu as pltpu
from jax.sharding import PartitionSpec as P

QUERY_HEADS = 64
KEY_VALUE_HEADS = 8
GROUP = QUERY_HEADS // KEY_VALUE_HEADS
HEAD_WIDTH = 128
STEP_COUNT = 4
PAGE_LENGTH = 32
PAGE_ROWS = 2 * PAGE_LENGTH
MAXP = 16
CAP = 2
VMEM_BYTES = 60 * 1024 * 1024


def pick_kernel(source, pages, outbox, sem):
    count = outbox.shape[0]
    for k in range(count):
        pltpu.make_async_copy(pages.at[source[k]], outbox.at[k], sem).start()
    pltpu.make_async_copy(pages.at[pl.ds(0, count)], outbox, sem).wait()


def pick(out_source, pages):
    shape = (out_source.shape[0],) + pages.shape[1:]
    return pl.pallas_call(
        pick_kernel,
        out_shape=jax.ShapeDtypeStruct(shape, pages.dtype),
        grid_spec=pltpu.PrefetchScalarGridSpec(
            num_scalar_prefetch=1,
            grid=(1,),
            in_specs=[pl.BlockSpec(memory_space=pl.ANY)],
            out_specs=pl.BlockSpec(shape, lambda i, s: (0, 0, 0)),
            scratch_shapes=[pltpu.SemaphoreType.DMA],
        ),
        name="pick",
    )(out_source, pages)


HALF_COUNT = 2


def layer_kernel(
    outbox, labels, local_table, lengths, queries, fresh, pages, up, weights, down,
    out,
    cands, inlab, tablev, table, outf, mixed, upall, everyone, part, lowpart,
    sendbuf, recvbuf, lowsend, lowrecv, sumsend, sumrecv, lowfull, extra,
    sent, got, lab_sent, lab_got, up_sent, up_got, ring_sent, ring_got, local_sem,
    s1_sent, s1_got, s2_sent, s2_got, relay_sent, relay_got, mate_sent, mate_got,
    main_sent, main_got, low_sent, low_got, sum_sent, sum_got,
):
    n, planes = upall.shape[0], upall.shape[1]
    me = lax.axis_index("req")
    lane = lax.axis_index("tp")
    core = lax.rem(me, 2)
    cx, cy = me // 8, lax.rem(me // 2, 4)
    first = cx * (1 - core) + cy * core
    second = cy * (1 - core) + cx * core
    above, below = lax.rem(lane + 1, planes), lax.rem(lane + planes - 1, planes)
    mate = me + 1 - 2 * core
    page_count = pages.shape[0]
    requests = fresh.shape[0]
    columns = out.shape[1]
    chunk_rows = queries.shape[0]
    half = chunk_rows // HALF_COUNT
    quarter = half // 2
    rank = HEAD_WIDTH // 2

    load = pltpu.make_async_copy(pages, cands.at[pl.ds(0, page_count)], local_sem.at[0])
    load.start()
    barrier = pltpu.get_barrier_semaphore()

    def greet(d, carry):
        pl.semaphore_signal(barrier, inc=1, device_id={"req": lax.rem(me + d, n)})
        return carry

    lax.fori_loop(1, n, greet, 0)
    pl.semaphore_signal(barrier, inc=1, device_id={"tp": above})
    pl.semaphore_signal(barrier, inc=1, device_id={"tp": below})
    inlab[me] = labels[me]
    pl.semaphore_wait(barrier, n + 1)

    def remote(src, dst, sent_sem, got_sem, **to):
        return pltpu.make_async_remote_copy(src, dst, sent_sem, got_sem, device_id=to)

    up_rows = upall.shape[2]

    def up_part(peer):
        return up.at[
            pl.ds(pl.multiple_of(lane * up_rows, up_rows), up_rows),
            pl.ds(pl.multiple_of(peer * columns, columns), columns),
        ]

    def label_copy(d):
        peer = lax.rem(me + d, n)
        return remote(
            labels.at[peer], inlab.at[me], lab_sent.at[d - 1], lab_got.at[d - 1], req=peer
        )

    def up_copy(d):
        peer = lax.rem(me + d, n)
        return remote(
            up_part(peer), upall.at[me, lane], up_sent.at[d - 1], up_got.at[d - 1], req=peer
        )

    def page_copy(d):
        peer = lax.rem(me + d, n)
        return remote(
            outbox.at[pl.ds(peer * CAP, CAP)],
            cands.at[pl.ds(page_count + me * CAP, CAP)],
            sent.at[d - 1],
            got.at[d - 1],
            req=peer,
        )

    own_up = pltpu.make_async_copy(up_part(me), upall.at[me, lane], local_sem.at[1])
    own_up.start()

    def begin_up(d, carry):
        label_copy(d).start()
        up_copy(d).start()
        return carry

    def begin_pages(d, carry):
        page_copy(d).start()
        return carry

    def finish_up(d, carry):
        up_copy(d).wait()
        return carry

    def finish_labels(d, carry):
        label_copy(d).wait()
        return carry

    def finish_pages(d, carry):
        page_copy(d).wait()
        return carry

    lax.fori_loop(1, n, begin_up, 0)
    lax.fori_loop(1, n, begin_pages, 0)

    hops = planes // 2

    def ring_copy(way, hop):
        peer = above if way == 0 else below
        origin = lax.rem(lane + planes + (hop if way == 1 else -hop), planes)
        piece = upall.at[:, origin]
        if hop == hops - 1:
            piece = upall.at[pl.ds(way * (n // 2), n // 2), origin]
        return pltpu.make_async_remote_copy(
            piece, piece, ring_sent.at[way, hop], ring_got.at[way, hop], device_id={"tp": peer}
        )

    def ring(hop):
        for way in range(2):
            if hop:
                ring_copy(way, hop - 1).wait_recv()
            if hop < hops:
                ring_copy(way, hop).start()

    lax.fori_loop(1, n, finish_up, 0)
    own_up.wait()
    ring(0)

    lax.fori_loop(1, n, finish_labels, 0)
    place = (
        lax.broadcasted_iota(jnp.int32, tablev.shape, 0) * HEAD_WIDTH
        + lax.broadcasted_iota(jnp.int32, tablev.shape, 1)
        + me * page_count
        + 1
    )

    def enter(source, entries):
        word = lax.shift_right_logical(inlab[source], jnp.full((1, HEAD_WIDTH), 6, jnp.int32))
        for k in range(CAP):
            index = page_count + source * CAP + k
            entries = entries + jnp.where(place == word[:, k : k + 1], index, 0)
        return entries

    tablev[...] = lax.fori_loop(0, n, enter, local_table[...])
    to_scalar = pltpu.make_async_copy(tablev, table, local_sem.at[2])
    to_scalar.start()
    lax.fori_loop(1, n // 2, finish_pages, 0)
    ring(1)
    lax.fori_loop(n // 2, n, finish_pages, 0)
    to_scalar.wait()
    load.wait()
    ring(2)

    old = MAXP * PAGE_ROWS
    width = old + HEAD_WIDTH
    rows_q = GROUP * STEP_COUNT
    column = lax.broadcasted_iota(jnp.int32, (rows_q, width), 1)
    step_of = lax.rem(lax.broadcasted_iota(jnp.int32, (rows_q, width), 0), STEP_COUNT)
    is_key = lax.rem(column, 2) == 0
    keep_new = is_key & (column >= old) & ((column - old) // 2 <= step_of)
    position = jnp.where(is_key & (column < old), column // 2, 1 << 20)
    scale = 1.0 / math.sqrt(HEAD_WIDTH)
    filler = jnp.zeros((HEAD_WIDTH - fresh.shape[1], HEAD_WIDTH), fresh.dtype)
    per_row = HEAD_WIDTH // MAXP

    def one(request, query):
        pieces = []
        for j in range(MAXP):
            page = table[request // per_row, lax.rem(request, per_row) * MAXP + j]
            pieces.append(cands[page])
        pieces.append(fresh[request])
        pieces.append(filler)
        stored = jnp.concatenate(pieces, axis=0)
        scores = (
            lax.dot_general(
                query, stored, (((1,), (1,)), ((), ())), preferred_element_type=jnp.float32
            )
            * scale
        )
        keep = keep_new | (position < lengths[request])
        scores = jnp.where(keep, scores, -jnp.inf)
        top = jnp.max(scores, axis=1, keepdims=True)
        exps = jnp.exp(scores - top)
        probs = exps / jnp.sum(exps, axis=1, keepdims=True)
        probs = pltpu.roll(probs, 1, 1).astype(jnp.bfloat16)
        return jnp.dot(probs, stored, preferred_element_type=jnp.float32)

    def pair(index, carry):
        base = pl.multiple_of(index * 2 * STEP_COUNT, 2 * STEP_COUNT)
        both_q = queries[pl.ds(base, 2 * STEP_COUNT), :].astype(jnp.float32)
        results = []
        for k in range(2):
            one_q = both_q[k * STEP_COUNT : (k + 1) * STEP_COUNT]
            query = jnp.concatenate(
                [one_q[:, h * HEAD_WIDTH : (h + 1) * HEAD_WIDTH] for h in range(GROUP)], axis=0
            ).astype(jnp.bfloat16)
            results.append(one(index * 2 + k, query))
        for h in range(GROUP):
            both = jnp.concatenate(
                [m[h * STEP_COUNT : (h + 1) * STEP_COUNT] for m in results], axis=0
            )
            outf[pl.ds(base, 2 * STEP_COUNT), h * HEAD_WIDTH : (h + 1) * HEAD_WIDTH] = both
        return carry

    def attend(start, stop):
        lax.fori_loop(start, stop, pair, 0)

    def spot(f, s, c):
        f, s = lax.rem(f + 8, 4), lax.rem(s + 8, 4)
        return f * (8 - 6 * c) + s * (2 + 6 * c) + c

    def at(df, ds):
        return spot(first + df, second + ds, core)

    def mate_at(df, ds):
        return spot(second + df, first + ds, 1 - core)

    OFFSET = (0, 1, -1, 2)
    DS = (0, -1, 1, 2)

    def whole(h):
        return pl.ds(h * half, half)

    def side_rows(h, way):
        return pl.ds(h * half + way * quarter, quarter)

    def step_one(h, way):
        to = at(1 if way == 0 else -1, 0)
        return remote(
            mixed.at[whole(h)], everyone.at[me, whole(h)],
            s1_sent.at[h, way], s1_got.at[h, way], req=to,
        )

    def step_one_half(h, way):
        ref = everyone.at[at(-1 if way == 0 else 1, 0), side_rows(h, way)]
        to = at(1 if way == 0 else -1, 0)
        return remote(ref, ref, s1_sent.at[h, 2 + way], s1_got.at[h, 2 + way], req=to)

    def step_two(h, k, way):
        ref = everyone.at[at(OFFSET[k], 0), whole(h)]
        src = mixed.at[whole(h)] if k == 0 else ref
        to = at(0, 1 if way == 0 else -1)
        return remote(src, ref, s2_sent.at[h, k, way], s2_got.at[h, k, way], req=to)

    def relay(h, k, way):
        ref = everyone.at[at(OFFSET[k], -1 if way == 0 else 1), side_rows(h, way)]
        to = at(0, 1 if way == 0 else -1)
        return remote(ref, ref, relay_sent.at[h, k, way], relay_got.at[h, k, way], req=to)

    def to_mate(h, k, j):
        ref = everyone.at[at(OFFSET[k], DS[j]), whole(h)]
        src = mixed.at[whole(h)] if k == 0 and j == 0 else ref
        return remote(src, ref, mate_sent.at[h, j, k], mate_got.at[h, j, k], req=mate)

    def arrived(ref, sem):
        pltpu.make_async_copy(ref, ref, sem).wait()

    def got_mate(h, k, j):
        arrived(everyone.at[mate_at(OFFSET[k], DS[j]), whole(h)], mate_got.at[h, j, k])

    def own_copy(h):
        return pltpu.make_async_copy(
            mixed.at[whole(h)], everyone.at[me, whole(h)], local_sem.at[3 + h]
        )

    def open_gather(h):
        rows = pl.ds(h * half, half)
        mixed[rows, :] = outf[rows, :].astype(mixed.dtype)
        for way in range(2):
            step_one(h, way).start()
        for way in range(2):
            step_two(h, 0, way).start()
        to_mate(h, 0, 0).start()
        own_copy(h).start()

    def pass_on(h, k):
        step_two(h, k, 0).start()
        step_two(h, k, 1).start()
        to_mate(h, k, 0).start()

    def near(h):
        for way, k in ((0, 2), (1, 1)):
            arrived(everyone.at[at(OFFSET[k], 0), whole(h)], s1_got.at[h, way])
            step_one_half(h, way).start()
            pass_on(h, k)

    def far(h):
        for way in range(2):
            arrived(everyone.at[at(2, 0), side_rows(h, way)], s1_got.at[h, 2 + way])
        pass_on(h, 3)

    def turn(h, k):
        for way, j in ((0, 1), (1, 2)):
            arrived(everyone.at[at(OFFSET[k], DS[j]), whole(h)], s2_got.at[h, k, way])
            relay(h, k, way).start()
            to_mate(h, k, j).start()

    def last(h, k):
        for way in range(2):
            arrived(everyone.at[at(OFFSET[k], 2), side_rows(h, way)], relay_got.at[h, k, way])
        to_mate(h, k, 3).start()

    row64 = lax.broadcasted_iota(jnp.int32, (half, HEAD_WIDTH), 0)
    col64 = lax.broadcasted_iota(jnp.int32, (half, HEAD_WIDTH), 1)
    narrow = lax.broadcasted_iota(jnp.int32, (quarter, HEAD_WIDTH), 1) < rank
    upper = col64 // rank

    def slot_column(r, h):
        values = (inlab[r] & 63).astype(jnp.float32)
        values = jnp.where(row64 + h * half == col64, values, 0.0)
        return jnp.sum(values, axis=1, keepdims=True).astype(jnp.int32)

    def batch(h, kjs):
        for k, j in kjs:
            got_mate(h, k, j)
        owners = [at(OFFSET[k], DS[j]) for k, j in kjs]
        owners += [mate_at(OFFSET[k], DS[j]) for k, j in kjs]
        rows = jnp.concatenate([everyone[r, whole(h)] for r in owners], axis=0)
        product = jnp.dot(rows, weights[...], preferred_element_type=jnp.float32)
        lows = jnp.dot(rows, down[...], preferred_element_type=jnp.float32)
        for i, r in enumerate(owners):
            cut = slice(i * half, (i + 1) * half)
            part[r, whole(h)] = product[cut]
            low = jnp.where(slot_column(r, h) == 2 * me + upper, lows[cut], 0.0)
            low = low + pltpu.roll(low, rank, 1)
            lowpart[r, h] = jnp.where(narrow, low[:quarter], low[quarter:])

    def batch_a(h):
        own_copy(h).wait()
        batch(h, [(k, 0) for k in range(4)])

    def batch_b(h, ks):
        batch(h, [(k, j) for k in ks for j in (1, 2)])

    def batch_c(h):
        batch(h, [(k, 3) for k in range(4)])

    subs = n // planes

    def target(way, step):
        return lax.rem(lane + planes + (step - hops if way == 0 else hops - step), planes)

    def low_copy(h, way, step):
        peer = below if way == 0 else above
        src, dst = lowsend.at[h, way, step], lowrecv.at[h, way, step]
        if step == 0:
            some = pl.ds(way * (subs // 2), subs // 2)
            src, dst = lowsend.at[h, way, step, some], lowrecv.at[h, way, step, some]
        return remote(src, dst, low_sent.at[h, way, step], low_got.at[h, way, step], tp=peer)

    def low_step(h, step):
        for way in range(2):
            if step:
                low_copy(h, way, step - 1).wait_recv()
            q = target(way, step)
            for sub in range(subs):
                mine = sub // (subs // 2) == way
                if step == 0 and not mine:
                    continue
                value = lowpart[q * subs + sub, h]
                if step > 1 or (step == 1 and mine):
                    value = value + lowrecv[h, way, step - 1, sub].astype(jnp.float32)
                lowsend[h, way, step, sub] = value.astype(jnp.bfloat16)
            low_copy(h, way, step).start()

    wing = columns // 2

    def main_copy(h, way, step, p):
        peer = below if way == 0 else above
        src, dst = sendbuf.at[h, way, step, p], recvbuf.at[h, way, step, p]
        if step == 0:
            side = pl.ds(way * wing, wing)
            src = sendbuf.at[h, way, step, p, :, :, side]
            dst = recvbuf.at[h, way, step, p, :, :, side]
        return remote(
            src, dst, main_sent.at[h, way, step, p], main_got.at[h, way, step, p], tp=peer
        )

    def main_step(h, step, p):
        for way in range(2):
            q = target(way, step)
            side = slice(way * wing, (way + 1) * wing)
            other = slice((1 - way) * wing, (2 - way) * wing)
            if step:
                main_copy(h, way, step - 1, p).wait_recv()
            for i in range(2):
                value = part[q * subs + 2 * p + i, whole(h)]
                if step == 0:
                    sendbuf[h, way, 0, p, i, :, side] = value[:, side].astype(jnp.bfloat16)
                elif step == 1:
                    came = recvbuf[h, way, 0, p, i, :, side].astype(jnp.float32)
                    sendbuf[h, way, 1, p, i, :, side] = (value[:, side] + came).astype(jnp.bfloat16)
                    sendbuf[h, way, 1, p, i, :, other] = value[:, other].astype(jnp.bfloat16)
                else:
                    came = recvbuf[h, way, step - 1, p, i].astype(jnp.float32)
                    sendbuf[h, way, step, p, i] = (value + came).astype(jnp.bfloat16)
            main_copy(h, way, step, p).start()

    def sum_mate():
        return remote(
            sumsend.at[0, 1 - core], sumrecv.at[0], sum_sent.at[0], sum_got.at[0], req=mate
        )

    def sum_axis(axis, d):
        peer = at(d, 0) if axis == 0 else at(0, d)
        i = 1 + 3 * axis + d - 1
        return remote(
            sumsend.at[1 + axis, 0], sumrecv.at[i], sum_sent.at[i], sum_got.at[i], req=peer
        )

    def sum_back():
        return remote(
            lowfull.at[core], lowfull.at[core], sum_sent.at[7], sum_got.at[7], req=mate
        )

    def low_end(h):
        for way in range(2):
            low_copy(h, way, hops - 1).wait_recv()
        for sub in range(subs):
            value = lowpart[lane * subs + sub, h]
            for way in range(2):
                value = value + lowrecv[h, way, hops - 1, sub].astype(jnp.float32)
            sumsend[0, h, pl.ds(quarter * sub, quarter)] = value.astype(jnp.bfloat16)

    def sum_first():
        sum_mate().wait_recv()
        value = sumsend[0, core].astype(jnp.float32) + sumrecv[0].astype(jnp.float32)
        sumsend[1, 0] = value.astype(jnp.bfloat16)
        for d in range(1, 4):
            sum_axis(0, d).start()

    def gathered(axis):
        value = sumsend[1 + axis, 0].astype(jnp.float32)
        for d in range(1, 4):
            sum_axis(axis, d).wait_recv()
            value = value + sumrecv[1 + 3 * axis + d - 1].astype(jnp.float32)
        return value.astype(jnp.bfloat16)

    def sum_second():
        sumsend[2, 0] = gathered(0)
        for d in range(1, 4):
            sum_axis(1, d).start()

    def sum_third():
        lowfull[core] = gathered(1)
        sum_back().start()

    def lora():
        arrived(lowfull.at[1 - core], sum_got.at[7])
        pieces, owners = [], []
        for sub in range(subs):
            for h in range(HALF_COUNT):
                packed = lowfull[h, pl.ds(quarter * sub, quarter)].astype(jnp.float32)
                turned = pltpu.roll(packed, rank, 1)
                pieces += [jnp.where(narrow, packed, turned), jnp.where(narrow, turned, packed)]
                owners.append(slot_column(lane * subs + sub, h))
        low = jnp.concatenate(pieces, axis=0)
        owner = jnp.concatenate(owners, axis=0)
        side = lax.broadcasted_iota(jnp.int32, low.shape, 1) // rank
        group = 8
        extra[...] = jnp.zeros(extra.shape, jnp.float32)

        def add(g, carry):
            wide = jnp.concatenate(
                [
                    jnp.where(owner == 2 * (g * group + m) + side, low, 0.0).astype(jnp.bfloat16)
                    for m in range(group)
                ],
                axis=1,
            )
            stored = upall[pl.ds(g * group, group)].reshape(group * planes * up_rows, columns)
            extra[...] += jnp.dot(wide, stored, preferred_element_type=jnp.float32)
            return carry

        lax.fori_loop(0, n // group, add, 0)

    pairs = requests // 2
    attend(0, pairs // 4)
    ring(3)
    attend(pairs // 4, pairs // 2)
    open_gather(0)
    attend(pairs // 2, pairs // 2 + 2)
    near(0)
    attend(pairs // 2 + 2, pairs // 2 + 4)
    turn(0, 0)
    far(0)
    attend(pairs // 2 + 4, pairs // 2 + 6)
    turn(0, 1)
    turn(0, 2)
    attend(pairs // 2 + 6, pairs)
    ring(4)
    open_gather(1)
    turn(0, 3)
    last(0, 0)
    batch_a(0)
    last(0, 1)
    near(1)
    batch_b(0, (0, 1))
    last(0, 2)
    last(0, 3)
    turn(1, 0)
    far(1)
    batch_b(0, (2, 3))
    turn(1, 1)
    batch_c(0)
    low_step(0, 0)
    main_step(0, 0, 0)
    main_step(0, 0, 1)
    turn(1, 2)
    low_step(0, 1)
    main_step(0, 1, 0)
    main_step(0, 1, 1)
    turn(1, 3)
    last(1, 0)
    batch_a(1)
    low_step(0, 2)
    main_step(0, 2, 0)
    last(1, 1)
    batch_b(1, (0, 1))
    main_step(0, 2, 1)
    low_step(0, 3)
    last(1, 2)
    last(1, 3)
    batch_b(1, (2, 3))
    main_step(0, 3, 0)
    main_step(0, 3, 1)
    batch_c(1)
    low_step(1, 0)
    low_end(0)
    main_step(1, 0, 0)
    main_step(1, 0, 1)
    low_step(1, 1)
    main_step(1, 1, 0)
    low_step(1, 2)
    main_step(1, 1, 1)
    low_step(1, 3)
    main_step(1, 2, 0)
    low_end(1)
    sum_mate().start()
    main_step(1, 2, 1)
    sum_first()
    main_step(1, 3, 0)
    sum_second()
    main_step(1, 3, 1)
    sum_third()
    lora()
    for h in range(HALF_COUNT):
        for sub in range(subs):
            p, i = sub // 2, sub % 2
            rows = pl.ds(sub * chunk_rows + h * half, half)
            value = part[lane * subs + sub, whole(h)] + extra[rows, :]
            for way in range(2):
                if i == 0:
                    main_copy(h, way, hops - 1, p).wait_recv()
                value = value + recvbuf[h, way, hops - 1, p, i].astype(jnp.float32)
            out[rows, :] = value.astype(out.dtype)

    for way in range(2):
        for hop in range(hops):
            ring_copy(way, hop).wait_send()
    for h in range(HALF_COUNT):
        for way in range(2):
            step_one(h, way).wait_send()
            step_one_half(h, way).wait_send()
            for k in range(4):
                step_two(h, k, way).wait_send()
                relay(h, k, way).wait_send()
            for step in range(hops):
                low_copy(h, way, step).wait_send()
                for p in range(2):
                    main_copy(h, way, step, p).wait_send()
        for k in range(4):
            for j in range(4):
                to_mate(h, k, j).wait_send()
    sum_mate().wait_send()
    for axis in range(2):
        for d in range(1, 4):
            sum_axis(axis, d).wait_send()
    sum_back().wait_send()


def layer(outbox, labels, local_table, lengths, queries, fresh, pages, up, weights, down, planes):
    rows, depth = queries.shape
    n, columns = labels.shape[0], weights.shape[1]
    hops, subs, half = planes // 2, n // planes, rows // HALF_COUNT
    hbm = pl.BlockSpec(memory_space=pltpu.HBM)
    vmem = pl.BlockSpec(memory_space=pltpu.VMEM)
    smem = pl.BlockSpec(memory_space=pltpu.SMEM)
    dma = pltpu.SemaphoreType.DMA
    bf16, f32, i32 = jnp.bfloat16, jnp.float32, jnp.int32
    hc = HALF_COUNT
    return pl.pallas_call(
        layer_kernel,
        out_shape=jax.ShapeDtypeStruct((n * rows // planes, columns), bf16),
        in_specs=[hbm, vmem, vmem, smem, vmem, vmem, hbm, hbm, vmem, vmem],
        out_specs=vmem,
        scratch_shapes=[
            pltpu.VMEM((pages.shape[0] + outbox.shape[0], PAGE_ROWS, HEAD_WIDTH), bf16),
            pltpu.VMEM(labels.shape, i32),
            pltpu.VMEM(local_table.shape, i32),
            pltpu.SMEM(local_table.shape, i32),
            pltpu.VMEM((rows, depth), f32),
            pltpu.VMEM((rows, depth), bf16),
            pltpu.VMEM((n, planes, up.shape[0] // planes, columns), bf16),
            pltpu.VMEM((n, rows, depth), bf16),
            pltpu.VMEM((n, rows, columns), f32),
            pltpu.VMEM((n, hc, half // 2, HEAD_WIDTH), f32),
            pltpu.VMEM((hc, 2, hops, 2, subs // 2, half, columns), bf16),
            pltpu.VMEM((hc, 2, hops, 2, subs // 2, half, columns), bf16),
            pltpu.VMEM((hc, 2, hops, subs, half // 2, HEAD_WIDTH), bf16),
            pltpu.VMEM((hc, 2, hops, subs, half // 2, HEAD_WIDTH), bf16),
            pltpu.VMEM((3, 2, rows, HEAD_WIDTH), bf16),
            pltpu.VMEM((7, rows, HEAD_WIDTH), bf16),
            pltpu.VMEM((2, rows, HEAD_WIDTH), bf16),
            pltpu.VMEM((n * rows // planes, columns), f32),
        ]
        + [dma((n - 1,))] * 6
        + [dma((2, hops))] * 2
        + [dma((5,))]
        + [dma((hc, 4))] * 2
        + [dma((hc, 4, 2))] * 4
        + [dma((hc, 4, 4))] * 2
        + [dma((hc, 2, hops, 2))] * 2
        + [dma((hc, 2, hops))] * 2
        + [dma((8,))] * 2,
        compiler_params=pltpu.CompilerParams(
            collective_id=0, has_side_effects=True, vmem_limit_bytes=VMEM_BYTES
        ),
        name="layer",
    )(outbox, labels, local_table, lengths, queries, fresh, pages, up, weights, down)


def on_device(
    queries,
    incoming_key_value,
    key_value_pages,
    page_request_home,
    lengths,
    request_adapter_index,
    adapter_storage_slot,
    adapter_down_factor,
    adapter_up_factor,
    output_projection_weight,
):
    n = lax.axis_size("req")
    tp_count = lax.axis_size("tp")
    me = lax.axis_index("req")
    per_dev = key_value_pages.shape[0]
    requests = lengths.shape[0]
    total = n * per_dev
    pages = key_value_pages.reshape(per_dev, PAGE_ROWS, HEAD_WIDTH)

    numbers = jnp.arange(per_dev, dtype=jnp.int32)
    peers = jnp.arange(n, dtype=jnp.int32)
    owner = page_request_home // per_dev
    match = (owner[:, None] == peers[None, :]) & (owner != me)[:, None]
    key = (numbers * total + page_request_home)[:, None]
    low_key = jnp.min(jnp.where(match, key, jnp.int32(2**30)), axis=0)
    high_key = jnp.max(jnp.where(match, key, -1), axis=0)
    keys = jnp.stack([low_key, high_key], axis=1)
    there = jnp.stack([high_key >= 0, high_key > low_key], axis=1)
    out_source = jnp.where(there, keys // total, 0).reshape(-1)
    out_label = jnp.where(there, keys % total, -1)

    slot_count = adapter_storage_slot.shape[0]
    slots = jnp.arange(slot_count, dtype=jnp.int32)
    own_slot = jnp.sum(
        jnp.where(
            request_adapter_index[:, None] == slots[None, :], adapter_storage_slot[None, :], 0
        ),
        axis=1,
    )
    token_slot = jnp.repeat(own_slot, STEP_COUNT)
    labels = (
        jnp.pad((out_label + 1) * 64, ((0, 0), (0, requests * STEP_COUNT - CAP)))
        + token_slot[None, :]
    ).reshape(n, 1, requests * STEP_COUNT)
    own_label = jnp.where(owner == me, page_request_home - me * per_dev, -1)
    local_table = jnp.sum(
        jnp.where(own_label[:, None] == numbers[None, :], numbers[:, None], 0), axis=0
    ).reshape(-1, HEAD_WIDTH)

    outbox = pick(out_source, pages)
    up = adapter_up_factor.reshape(-1, adapter_up_factor.shape[2])
    fresh = jnp.transpose(incoming_key_value, (1, 0, 2)).reshape(
        requests, 2 * STEP_COUNT, HEAD_WIDTH
    )
    fresh = jnp.pad(fresh, ((0, 0), (0, 8), (0, 0)))
    own_adapters, _, rank = adapter_down_factor.shape
    down = jnp.transpose(adapter_down_factor, (1, 0, 2)).reshape(-1, own_adapters * rank)
    return layer(
        outbox, labels, local_table, lengths, queries, fresh, pages, up,
        output_projection_weight, down, tp_count,
    )


def solution(mesh):
    return jax.shard_map(
        on_device,
        mesh=mesh,
        in_specs=(
            P("req", "tp"),
            P(None, "req", "tp"),
            P("req", None, None, "tp"),
            P("req"),
            P("req"),
            P("req"),
            P(),
            P("req", "tp", None),
            P("req", None, None),
            P("tp", "req"),
        ),
        out_specs=P("tp", "req"),
        check_vma=False,
    )
```

time: 351 us -> 136 us (0.39)
  waiting for transfers between devices: 262 us -> 0 us
  Pallas kernels: 50.4 us -> 127 us
  between operations: 13.4 us -> 0.06 us
  matrix products: 10.4 us -> 0 us
  local copies, waits for them, and re-layouts: 10.5 us -> 5.78 us
    psum x1 -> x0, waiting for transfers between devices: 115 us -> none  [on_device(): low = lax.psum(low, 'req')]
    all_gather x2 -> x0, waiting for transfers between devices: 103 us -> none  [the longest x1 64.1 us: on_device(): everyone = lax.all_gather(mixed, 'req', axis=0, tiled=True)]
    pallas_call x3 -> x2, Pallas kernels: 50.4 us -> 127 us  [the longest x1 123 us: layer(): pl.pallas_call(layer_kernel, out_shape=jax.ShapeDtypeStruct((n * rows //...]
    reduce_scatter x1 -> x0, waiting for transfers between devices: 42.4 us -> none  [on_device(): reduced = lax.psum_scatter(partial, 'tp', scatter_dimension=0, tiled=True)]
    dot_general x2 -> x0, matrix products: 10.4 us -> none  [the longest x1 8.35 us: on_device(): product = jnp.dot(everyone, weights, preferred_element_type=jnp.float32)]
  transfers between devices with their start and end apart: 4 -> 0, of which waited for: 4 -> 0; matrix products, arithmetic and copies ran while one was open for 1% -> 0% of each run, Pallas kernels for 0% -> 0%
where the time goes in v3:
time: 136 us
  Pallas kernels  127 us (93%)
  local copies, waits for them, and re-layouts  5.78 us (4%)
  other arithmetic  3.71 us (3%)
    pallas_call x1, Pallas kernels, layer(): pl.pallas_call(layer_kernel, out_shape=jax.ShapeDtypeStruct((n * rows //...  123 us
    pallas_call x1, Pallas kernels, pick(): pl.pallas_call(pick_kernel, out_shape=jax.ShapeDtypeStruct(shape, pages.d...  3.74 us

profile of v3, /device:TPU:1, one launch (start us, length us, event | category | flops | bytes accessed | tf_op | source)
XLA Modules:
  0.0 136.2 jit_solution(9068550927674691725)
XLA Ops:
  0.0 0.8 select_reduce_fusion.3
  0.9 0.7 subtract_select_fusion
  1.6 0.8 select_reduce_fusion
  2.3 0.1 select_reduce_fusion.2
  2.5 0.1 copy.46
  2.6 0.1 stack.17
  2.7 0.1 copy.50
  2.8 0.1 copy.45
  2.9 0.1 stack.15
  3.0 0.6 fusion.4.source
  3.6 0.1 copy.51
  3.7 0.1 broadcast_in_dim.72
  3.8 0.1 add.33
  3.9 0.6 pad_add_fusion
  4.5 0.9 copy.53
  5.4 0.7 pad.9.fresh
  6.1 1.8 %copy.54.down = bf16[1024,128]{1,0:T(8,128)(2,1)} copy(bf16[1024,128]{0,1:T(8,128)(2,1)} %bitcast.18) | data formatting | bytes 524288 | tf_op jit(solution)/shard_map/reshape | solution.py:733
  7.9 3.7 %pick.1.outbox = bf16[64,64,128]{2,1,0:T(8,128)(2,1)} custom-call(s32[64]{0:T(128)} %fusion.4.source, bf16[512,64,128]{2,1,0:T(8,128)(2,1)} %bitcast.14), custom_call_target="tpu_custom_call" | custom-call | tf_op jit(solution)/shard_map/pick/pallas_call | solution.py:32
  11.6 122.9 %layer.1 = bf16[512,256]{1,0:T(8,128)(2,1)} custom-call(bf16[64,64,128]{2,1,0:T(8,128)(2,1)} %pick.1.outbox, s32[32,1,128]{2,1,0:T(1,128)} %bitcast.19, s32[4,128]{1,0:T(4,128)} %bitcast.21, s32[32]{0:T(128)} %lengths.1, bf16[128,1024]{1,0:T(8,128)(2,1)} %queries.1, bf16[32,16,128]{2,1,0:T(8,128)(2,1)} %pad.9.fresh, bf16[512,64,128]{2,1,0:T(8,128)(2,1)} %bitcast.15, ...), custom_call_target="tpu_custom_call" | custom-call | tf_op jit(solution)/shard_map/layer/pallas_call | solution.py:635
  134.5 1.7 %copy.56 = bf16[512,256]{1,0:T(8,128)(2,1)} copy(bf16[512,256]{1,0:T(8,128)(2,1)} %layer.1) | data formatting | bytes 524288
  (6 shorter events, 0.1 us)

commit v4 on v3

--- a/solution.py
+++ b/solution.py
@@ -20,38 +20,15 @@
 VMEM_BYTES = 60 * 1024 * 1024
 
 
-def pick_kernel(source, pages, outbox, sem):
-    count = outbox.shape[0]
-    for k in range(count):
-        pltpu.make_async_copy(pages.at[source[k]], outbox.at[k], sem).start()
-    pltpu.make_async_copy(pages.at[pl.ds(0, count)], outbox, sem).wait()
-
-
-def pick(out_source, pages):
-    shape = (out_source.shape[0],) + pages.shape[1:]
-    return pl.pallas_call(
-        pick_kernel,
-        out_shape=jax.ShapeDtypeStruct(shape, pages.dtype),
-        grid_spec=pltpu.PrefetchScalarGridSpec(
-            num_scalar_prefetch=1,
-            grid=(1,),
-            in_specs=[pl.BlockSpec(memory_space=pl.ANY)],
-            out_specs=pl.BlockSpec(shape, lambda i, s: (0, 0, 0)),
-            scratch_shapes=[pltpu.SemaphoreType.DMA],
-        ),
-        name="pick",
-    )(out_source, pages)
-
-
 HALF_COUNT = 2
 
 
 def layer_kernel(
-    outbox, labels, local_table, lengths, queries, fresh, pages, up, weights, down,
+    home, home_s, adapter, storage, lengths, queries, incoming, pages, up, weights, down,
     out,
-    cands, inlab, tablev, table, outf, mixed, upall, everyone, part, lowpart,
-    sendbuf, recvbuf, lowsend, lowrecv, sumsend, sumrecv, lowfull, extra,
-    sent, got, lab_sent, lab_got, up_sent, up_got, ring_sent, ring_got, local_sem,
+    cands, inbox, outbox, labels, inlab, sourcev, sources, tablev, table, outf, mixed, upall,
+    everyone, part, lowpart, sendbuf, recvbuf, lowsend, lowrecv, sumsend, sumrecv, lowfull, extra,
+    many_sent, many_got, ring_sent, ring_got, local_sem,
     s1_sent, s1_got, s2_sent, s2_got, relay_sent, relay_got, mate_sent, mate_got,
     main_sent, main_got, low_sent, low_got, sum_sent, sum_got,
 ):
@@ -65,7 +42,7 @@
     above, below = lax.rem(lane + 1, planes), lax.rem(lane + planes - 1, planes)
     mate = me + 1 - 2 * core
     page_count = pages.shape[0]
-    requests = fresh.shape[0]
+    requests = lengths.shape[0]
     columns = out.shape[1]
     chunk_rows = queries.shape[0]
     half = chunk_rows // HALF_COUNT
@@ -83,11 +60,68 @@
     lax.fori_loop(1, n, greet, 0)
     pl.semaphore_signal(barrier, inc=1, device_id={"tp": above})
     pl.semaphore_signal(barrier, inc=1, device_id={"tp": below})
-    inlab[me] = labels[me]
-    pl.semaphore_wait(barrier, n + 1)
 
     def remote(src, dst, sent_sem, got_sem, **to):
         return pltpu.make_async_remote_copy(src, dst, sent_sem, got_sem, device_id=to)
+
+    def arrived(ref, sem):
+        pltpu.make_async_copy(ref, ref, sem).wait()
+
+    shift = n * page_count
+    bits = shift.bit_length() - 1
+    page_bits = page_count.bit_length() - 1
+    peer_row = lax.broadcasted_iota(jnp.int32, (n, HEAD_WIDTH), 0)
+    lane_of = lax.broadcasted_iota(jnp.int32, (n, HEAD_WIDTH), 1)
+    low_key = jnp.full((n, HEAD_WIDTH), 2 * page_count * shift, jnp.int32)
+    high_key = jnp.full((n, HEAD_WIDTH), -1, jnp.int32)
+    for i in range(page_count // HEAD_WIDTH):
+        homes = jnp.broadcast_to(home[i : i + 1, :], (n, HEAD_WIDTH))
+        match = (homes >> page_bits == peer_row) & (peer_row != me)
+        key = (lane_of + i * HEAD_WIDTH) * shift + homes
+        low_key = jnp.where(match, jnp.minimum(low_key, key), low_key)
+        high_key = jnp.where(match, jnp.maximum(high_key, key), high_key)
+    least = jnp.min(low_key, axis=1, keepdims=True)
+    most = jnp.max(high_key, axis=1, keepdims=True)
+    chosen = jnp.where(lane_of == 0, least, most)
+    there = ((lane_of == 0) & (most >= 0)) | ((lane_of == 1) & (most > least))
+    sourcev[...] = jnp.where(there, jnp.clip(chosen >> bits, 0, page_count - 1), 0)
+    to_sources = pltpu.make_async_copy(sourcev, sources, local_sem.at[5])
+    to_sources.start()
+    words = jnp.where(there, ((chosen & (shift - 1)) + 1) * 64, 0)
+    token_lane = lax.broadcasted_iota(jnp.int32, (1, HEAD_WIDTH), 1)
+    slots = jnp.zeros((1, HEAD_WIDTH), jnp.int32)
+    for i in range(requests):
+        slots = jnp.where(token_lane // STEP_COUNT == i, storage[adapter[i]], slots)
+    for i in range(n):
+        labels[i] = words[i : i + 1] + slots
+    inlab[me] = slots
+
+    place = (
+        lax.broadcasted_iota(jnp.int32, tablev.shape, 0) * HEAD_WIDTH
+        + lax.broadcasted_iota(jnp.int32, tablev.shape, 1)
+        + me * page_count
+    )
+    run = 16
+
+    def enter_own(i, entries):
+        for u in range(run):
+            at_home = home_s[i // (HEAD_WIDTH // run), lax.rem(i, HEAD_WIDTH // run) * run + u]
+            entries = jnp.where(place == at_home, i * run + u, entries)
+        return entries
+
+    own_table = lax.fori_loop(
+        0, page_count // run, enter_own, jnp.zeros(tablev.shape, jnp.int32)
+    )
+    to_sources.wait()
+    load.wait()
+
+    def pick(d, carry):
+        for k in range(CAP):
+            outbox[d * CAP + k] = cands[sources[d, k]]
+        return carry
+
+    lax.fori_loop(0, n, pick, 0)
+    pl.semaphore_wait(barrier, n + 1)
 
     up_rows = upall.shape[2]
 
@@ -99,52 +133,45 @@
 
     def label_copy(d):
         peer = lax.rem(me + d, n)
-        return remote(
-            labels.at[peer], inlab.at[me], lab_sent.at[d - 1], lab_got.at[d - 1], req=peer
-        )
-
-    def up_copy(d):
-        peer = lax.rem(me + d, n)
-        return remote(
-            up_part(peer), upall.at[me, lane], up_sent.at[d - 1], up_got.at[d - 1], req=peer
-        )
+        return remote(labels.at[peer], inlab.at[me], many_sent.at[0], many_got.at[0], req=peer)
 
     def page_copy(d):
         peer = lax.rem(me + d, n)
         return remote(
             outbox.at[pl.ds(peer * CAP, CAP)],
-            cands.at[pl.ds(page_count + me * CAP, CAP)],
-            sent.at[d - 1],
-            got.at[d - 1],
+            inbox.at[pl.ds(me * CAP, CAP)],
+            many_sent.at[1],
+            many_got.at[1],
             req=peer,
+        )
+
+    def up_copy(d):
+        peer = lax.rem(me + d, n)
+        return remote(
+            up_part(peer), upall.at[me, lane], many_sent.at[2], many_got.at[2], req=peer
         )
 
     own_up = pltpu.make_async_copy(up_part(me), upall.at[me, lane], local_sem.at[1])
     own_up.start()
 
-    def begin_up(d, carry):
+    def begin_labels(d, carry):
         label_copy(d).start()
-        up_copy(d).start()
         return carry
 
     def begin_pages(d, carry):
         page_copy(d).start()
         return carry
 
-    def finish_up(d, carry):
-        up_copy(d).wait()
+    def begin_up(d, carry):
+        up_copy(d).start()
         return carry
 
-    def finish_labels(d, carry):
-        label_copy(d).wait()
-        return carry
-
-    def finish_pages(d, carry):
-        page_copy(d).wait()
-        return carry
-
+    lax.fori_loop(1, n, begin_labels, 0)
+    lax.fori_loop(1, n, begin_pages, 0)
     lax.fori_loop(1, n, begin_up, 0)
-    lax.fori_loop(1, n, begin_pages, 0)
+    all_labels = inlab.at[pl.ds(0, n - 1)]
+    all_pages = inbox.at[pl.ds(0, (n - 1) * CAP)]
+    all_up = upall.at[pl.ds(0, n - 1), 0]
 
     hops = planes // 2
 
@@ -165,34 +192,26 @@
             if hop < hops:
                 ring_copy(way, hop).start()
 
-    lax.fori_loop(1, n, finish_up, 0)
+    arrived(all_labels, many_got.at[0])
+    entries = own_table
+    for source in range(n):
+        word = inlab[source] >> 6
+        for k in range(CAP):
+            index = page_count + source * CAP + k
+            entries = jnp.where(place + 1 == word[:, k : k + 1], index, entries)
+    tablev[...] = entries
+    to_scalar = pltpu.make_async_copy(tablev, table, local_sem.at[2])
+    to_scalar.start()
+    arrived(all_pages, many_got.at[1])
+    take_in = pltpu.make_async_copy(
+        inbox, cands.at[pl.ds(page_count, n * CAP)], local_sem.at[0]
+    )
+    take_in.start()
+    arrived(all_up, many_got.at[2])
     own_up.wait()
     ring(0)
-
-    lax.fori_loop(1, n, finish_labels, 0)
-    place = (
-        lax.broadcasted_iota(jnp.int32, tablev.shape, 0) * HEAD_WIDTH
-        + lax.broadcasted_iota(jnp.int32, tablev.shape, 1)
-        + me * page_count
-        + 1
-    )
-
-    def enter(source, entries):
-        word = lax.shift_right_logical(inlab[source], jnp.full((1, HEAD_WIDTH), 6, jnp.int32))
-        for k in range(CAP):
-            index = page_count + source * CAP + k
-            entries = entries + jnp.where(place == word[:, k : k + 1], index, 0)
-        return entries
-
-    tablev[...] = lax.fori_loop(0, n, enter, local_table[...])
-    to_scalar = pltpu.make_async_copy(tablev, table, local_sem.at[2])
-    to_scalar.start()
-    lax.fori_loop(1, n // 2, finish_pages, 0)
-    ring(1)
-    lax.fori_loop(n // 2, n, finish_pages, 0)
     to_scalar.wait()
-    load.wait()
-    ring(2)
+    take_in.wait()
 
     old = MAXP * PAGE_ROWS
     width = old + HEAD_WIDTH
@@ -200,18 +219,21 @@
     column = lax.broadcasted_iota(jnp.int32, (rows_q, width), 1)
     step_of = lax.rem(lax.broadcasted_iota(jnp.int32, (rows_q, width), 0), STEP_COUNT)
     is_key = lax.rem(column, 2) == 0
-    keep_new = is_key & (column >= old) & ((column - old) // 2 <= step_of)
+    fresh_at = column - old
+    keep_new = [
+        (fresh_at >= k * STEP_COUNT) & (fresh_at - k * STEP_COUNT <= step_of) for k in range(2)
+    ]
     position = jnp.where(is_key & (column < old), column // 2, 1 << 20)
     scale = 1.0 / math.sqrt(HEAD_WIDTH)
-    filler = jnp.zeros((HEAD_WIDTH - fresh.shape[1], HEAD_WIDTH), fresh.dtype)
+    filler = jnp.zeros((HEAD_WIDTH - 4 * STEP_COUNT, HEAD_WIDTH), cands.dtype)
     per_row = HEAD_WIDTH // MAXP
 
-    def one(request, query):
+    def one(request, query, fresh, keep_fresh):
         pieces = []
         for j in range(MAXP):
             page = table[request // per_row, lax.rem(request, per_row) * MAXP + j]
             pieces.append(cands[page])
-        pieces.append(fresh[request])
+        pieces.append(fresh)
         pieces.append(filler)
         stored = jnp.concatenate(pieces, axis=0)
         scores = (
@@ -220,24 +242,34 @@
             )
             * scale
         )
-        keep = keep_new | (position < lengths[request])
+        keep = keep_fresh | (position < lengths[request])
         scores = jnp.where(keep, scores, -jnp.inf)
         top = jnp.max(scores, axis=1, keepdims=True)
         exps = jnp.exp(scores - top)
         probs = exps / jnp.sum(exps, axis=1, keepdims=True)
-        probs = pltpu.roll(probs, 1, 1).astype(jnp.bfloat16)
+        probs = jnp.concatenate(
+            [
+                pltpu.roll(probs[:, :old], 1, 1),
+                pltpu.roll(probs[:, old:], 2 * STEP_COUNT, 1),
+            ],
+            axis=1,
+        ).astype(jnp.bfloat16)
         return jnp.dot(probs, stored, preferred_element_type=jnp.float32)
 
     def pair(index, carry):
         base = pl.multiple_of(index * 2 * STEP_COUNT, 2 * STEP_COUNT)
         both_q = queries[pl.ds(base, 2 * STEP_COUNT), :].astype(jnp.float32)
+        fresh = jnp.concatenate(
+            [incoming[i, pl.ds(base, 2 * STEP_COUNT), :].astype(jnp.float32) for i in range(2)],
+            axis=0,
+        ).astype(jnp.bfloat16)
         results = []
         for k in range(2):
             one_q = both_q[k * STEP_COUNT : (k + 1) * STEP_COUNT]
             query = jnp.concatenate(
                 [one_q[:, h * HEAD_WIDTH : (h + 1) * HEAD_WIDTH] for h in range(GROUP)], axis=0
             ).astype(jnp.bfloat16)
-            results.append(one(index * 2 + k, query))
+            results.append(one(index * 2 + k, query, fresh, keep_new[k]))
         for h in range(GROUP):
             both = jnp.concatenate(
                 [m[h * STEP_COUNT : (h + 1) * STEP_COUNT] for m in results], axis=0
@@ -294,9 +326,6 @@
         ref = everyone.at[at(OFFSET[k], DS[j]), whole(h)]
         src = mixed.at[whole(h)] if k == 0 and j == 0 else ref
         return remote(src, ref, mate_sent.at[h, j, k], mate_got.at[h, j, k], req=mate)
-
-    def arrived(ref, sem):
-        pltpu.make_async_copy(ref, ref, sem).wait()
 
     def got_mate(h, k, j):
         arrived(everyone.at[mate_at(OFFSET[k], DS[j]), whole(h)], mate_got.at[h, j, k])
@@ -360,7 +389,9 @@
         owners += [mate_at(OFFSET[k], DS[j]) for k, j in kjs]
         rows = jnp.concatenate([everyone[r, whole(h)] for r in owners], axis=0)
         product = jnp.dot(rows, weights[...], preferred_element_type=jnp.float32)
-        lows = jnp.dot(rows, down[...], preferred_element_type=jnp.float32)
+        lows = lax.dot_general(
+            rows, down[...], (((1,), (1,)), ((), ())), preferred_element_type=jnp.float32
+        )
         for i, r in enumerate(owners):
             cut = slice(i * half, (i + 1) * half)
             part[r, whole(h)] = product[cut]
@@ -518,10 +549,9 @@
         lax.fori_loop(0, n // group, add, 0)
 
     pairs = requests // 2
-    attend(0, pairs // 4)
-    ring(3)
-    attend(pairs // 4, pairs // 2)
+    attend(0, pairs // 2)
     open_gather(0)
+    ring(1)
     attend(pairs // 2, pairs // 2 + 2)
     near(0)
     attend(pairs // 2 + 2, pairs // 2 + 4)
@@ -531,14 +561,15 @@
     turn(0, 1)
     turn(0, 2)
     attend(pairs // 2 + 6, pairs)
-    ring(4)
     open_gather(1)
+    ring(2)
     turn(0, 3)
     last(0, 0)
     batch_a(0)
     last(0, 1)
     near(1)
     batch_b(0, (0, 1))
+    ring(3)
     last(0, 2)
     last(0, 3)
     turn(1, 0)
@@ -586,6 +617,7 @@
     sum_second()
     main_step(1, 3, 1)
     sum_third()
+    ring(4)
     lora()
     for h in range(HALF_COUNT):
         for sub in range(subs):
@@ -598,6 +630,9 @@
                 value = value + recvbuf[h, way, hops - 1, p, i].astype(jnp.float32)
             out[rows, :] = value.astype(out.dtype)
 
+    arrived(all_labels, many_sent.at[0])
+    arrived(all_pages, many_sent.at[1])
+    arrived(all_up, many_sent.at[2])
     for way in range(2):
         for hop in range(hops):
             ring_copy(way, hop).wait_send()
@@ -622,9 +657,9 @@
     sum_back().wait_send()
 
 
-def layer(outbox, labels, local_table, lengths, queries, fresh, pages, up, weights, down, planes):
+def layer(n, planes, home, adapter, storage, lengths, queries, incoming, pages, up, weights, down):
     rows, depth = queries.shape
-    n, columns = labels.shape[0], weights.shape[1]
+    columns = weights.shape[1]
     hops, subs, half = planes // 2, n // planes, rows // HALF_COUNT
     hbm = pl.BlockSpec(memory_space=pltpu.HBM)
     vmem = pl.BlockSpec(memory_space=pltpu.VMEM)
@@ -635,13 +670,18 @@
     return pl.pallas_call(
         layer_kernel,
         out_shape=jax.ShapeDtypeStruct((n * rows // planes, columns), bf16),
-        in_specs=[hbm, vmem, vmem, smem, vmem, vmem, hbm, hbm, vmem, vmem],
+        in_specs=[vmem, smem, smem, smem, smem, vmem, vmem, hbm, hbm, vmem, vmem],
         out_specs=vmem,
         scratch_shapes=[
-            pltpu.VMEM((pages.shape[0] + outbox.shape[0], PAGE_ROWS, HEAD_WIDTH), bf16),
-            pltpu.VMEM(labels.shape, i32),
-            pltpu.VMEM(local_table.shape, i32),
-            pltpu.SMEM(local_table.shape, i32),
+            pltpu.VMEM((pages.shape[0] + n * CAP, PAGE_ROWS, HEAD_WIDTH), bf16),
+            pltpu.VMEM((n * CAP, PAGE_ROWS, HEAD_WIDTH), bf16),
+            pltpu.VMEM((n * CAP, PAGE_ROWS, HEAD_WIDTH), bf16),
+            pltpu.VMEM((n, 1, HEAD_WIDTH), i32),
+            pltpu.VMEM((n, 1, HEAD_WIDTH), i32),
+            pltpu.VMEM((n, HEAD_WIDTH), i32),
+            pltpu.SMEM((n, HEAD_WIDTH), i32),
+            pltpu.VMEM(home.shape, i32),
+            pltpu.SMEM(home.shape, i32),
             pltpu.VMEM((rows, depth), f32),
             pltpu.VMEM((rows, depth), bf16),
             pltpu.VMEM((n, planes, up.shape[0] // planes, columns), bf16),
@@ -657,9 +697,9 @@
             pltpu.VMEM((2, rows, HEAD_WIDTH), bf16),
             pltpu.VMEM((n * rows // planes, columns), f32),
         ]
-        + [dma((n - 1,))] * 6
+        + [dma((3,))] * 2
         + [dma((2, hops))] * 2
-        + [dma((5,))]
+        + [dma((6,))]
         + [dma((hc, 4))] * 2
         + [dma((hc, 4, 2))] * 4
         + [dma((hc, 4, 4))] * 2
@@ -670,7 +710,7 @@
             collective_id=0, has_side_effects=True, vmem_limit_bytes=VMEM_BYTES
         ),
         name="layer",
-    )(outbox, labels, local_table, lengths, queries, fresh, pages, up, weights, down)
+    )(home, home, adapter, storage, lengths, queries, incoming, pages, up, weights, down)
 
 
 def on_device(
@@ -685,55 +725,21 @@
     adapter_up_factor,
     output_projection_weight,
 ):
-    n = lax.axis_size("req")
-    tp_count = lax.axis_size("tp")
-    me = lax.axis_index("req")
     per_dev = key_value_pages.shape[0]
-    requests = lengths.shape[0]
-    total = n * per_dev
-    pages = key_value_pages.reshape(per_dev, PAGE_ROWS, HEAD_WIDTH)
-
-    numbers = jnp.arange(per_dev, dtype=jnp.int32)
-    peers = jnp.arange(n, dtype=jnp.int32)
-    owner = page_request_home // per_dev
-    match = (owner[:, None] == peers[None, :]) & (owner != me)[:, None]
-    key = (numbers * total + page_request_home)[:, None]
-    low_key = jnp.min(jnp.where(match, key, jnp.int32(2**30)), axis=0)
-    high_key = jnp.max(jnp.where(match, key, -1), axis=0)
-    keys = jnp.stack([low_key, high_key], axis=1)
-    there = jnp.stack([high_key >= 0, high_key > low_key], axis=1)
-    out_source = jnp.where(there, keys // total, 0).reshape(-1)
-    out_label = jnp.where(there, keys % total, -1)
-
-    slot_count = adapter_storage_slot.shape[0]
-    slots = jnp.arange(slot_count, dtype=jnp.int32)
-    own_slot = jnp.sum(
-        jnp.where(
-            request_adapter_index[:, None] == slots[None, :], adapter_storage_slot[None, :], 0
-        ),
-        axis=1,
-    )
-    token_slot = jnp.repeat(own_slot, STEP_COUNT)
-    labels = (
-        jnp.pad((out_label + 1) * 64, ((0, 0), (0, requests * STEP_COUNT - CAP)))
-        + token_slot[None, :]
-    ).reshape(n, 1, requests * STEP_COUNT)
-    own_label = jnp.where(owner == me, page_request_home - me * per_dev, -1)
-    local_table = jnp.sum(
-        jnp.where(own_label[:, None] == numbers[None, :], numbers[:, None], 0), axis=0
-    ).reshape(-1, HEAD_WIDTH)
-
-    outbox = pick(out_source, pages)
-    up = adapter_up_factor.reshape(-1, adapter_up_factor.shape[2])
-    fresh = jnp.transpose(incoming_key_value, (1, 0, 2)).reshape(
-        requests, 2 * STEP_COUNT, HEAD_WIDTH
-    )
-    fresh = jnp.pad(fresh, ((0, 0), (0, 8), (0, 0)))
-    own_adapters, _, rank = adapter_down_factor.shape
-    down = jnp.transpose(adapter_down_factor, (1, 0, 2)).reshape(-1, own_adapters * rank)
+    own_adapters, depth, rank = adapter_down_factor.shape
     return layer(
-        outbox, labels, local_table, lengths, queries, fresh, pages, up,
-        output_projection_weight, down, tp_count,
+        lax.axis_size("req"),
+        lax.axis_size("tp"),
+        page_request_home.reshape(-1, HEAD_WIDTH),
+        request_adapter_index,
+        adapter_storage_slot,
+        lengths,
+        queries,
+        incoming_key_value,
+        key_value_pages.reshape(per_dev, PAGE_ROWS, HEAD_WIDTH),
+        adapter_up_factor.reshape(-1, adapter_up_factor.shape[2]),
+        output_projection_weight,
+        jnp.transpose(adapter_down_factor, (0, 2, 1)).reshape(own_adapters * rank, depth),
     )
 
 

time: 136 us -> 111 us (0.82)
  Pallas kernels: 127 us -> 109 us
  local copies, waits for them, and re-layouts: 5.78 us -> 1.67 us
  other arithmetic: 3.71 us -> 0 us
    pallas_call x1, Pallas kernels: 123 us -> 109 us  [layer(): pl.pallas_call(layer_kernel, out_shape=jax.ShapeDtypeStruct((n * rows //...]
    pallas_call x1 -> x0, Pallas kernels: 3.74 us -> none  [pick(): pl.pallas_call(pick_kernel, out_shape=jax.ShapeDtypeStruct(shape, pages.d...]
    reshape x1 -> x0, local copies, waits for them, and re-layouts: 1.79 us -> none  [on_device(): jnp.transpose(adapter_down_factor, (1, 0, 2))]
    reduce_sum x2 -> x0, other arithmetic: 1.61 us -> none  [the longest x1 0.85 us: on_device(): jnp.sum(jnp.where(request_adapter_index[:, None] == slots[None, :], adapt...]
where the time goes in v4:
time: 111 us
  Pallas kernels  109 us (98%)
  local copies, waits for them, and re-layouts  1.67 us (2%)
    pallas_call x1, Pallas kernels, layer(): pl.pallas_call(layer_kernel, out_shape=jax.ShapeDtypeStruct((n * rows //...  109 us

profile of v4, /device:TPU:1, one launch (start us, length us, event | category | flops | bytes accessed | tf_op | source)
XLA Modules:
  0.0 111.0 jit_solution(11583875277711444622)
XLA Ops:
  0.0 109.3 %layer.1 = bf16[512,256]{1,0:T(8,128)(2,1)} custom-call(s32[4,128]{1,0:T(4,128)} %bitcast.9, s32[4,128]{1,0:T(4,128)} %bitcast.10, s32[32]{0:T(128)} %adapter.1, s32[64]{0:T(128)} %storage.1, s32[32]{0:T(128)} %lengths.1, bf16[128,1024]{1,0:T(8,128)(2,1)} %queries.1, bf16[2,128,128]{2,1,0:T(8,128)(2,1)} %incoming.1, bf16[512,64,128]{2,1,0:T(8,128)(2,1)} %bitcast.6, ...), custom_call_target="tpu_custom_call" | custom-call | tf_op jit(solution)/shard_map/layer/pallas_call | solution.py:670
  109.4 1.7 %copy.12 = bf16[512,256]{1,0:T(8,128)(2,1)} copy(bf16[512,256]{1,0:T(8,128)(2,1)} %layer.1) | data formatting | bytes 524288

commit v5 on v4

--- a/solution.py
+++ b/solution.py
@@ -27,10 +27,10 @@
     home, home_s, adapter, storage, lengths, queries, incoming, pages, up, weights, down,
     out,
     cands, inbox, outbox, labels, inlab, sourcev, sources, tablev, table, outf, mixed, upall,
-    everyone, part, lowpart, sendbuf, recvbuf, lowsend, lowrecv, sumsend, sumrecv, lowfull, extra,
+    everyone, part, sendbuf, recvbuf, lowsend, lowrecv, lowsum, lowz, lowfull, extra,
     many_sent, many_got, ring_sent, ring_got, local_sem,
     s1_sent, s1_got, s2_sent, s2_got, relay_sent, relay_got, mate_sent, mate_got,
-    main_sent, main_got, low_sent, low_got, sum_sent, sum_got,
+    main_sent, main_got, low_sent, low_got, full_got,
 ):
     n, planes = upall.shape[0], upall.shape[1]
     me = lax.axis_index("req")
@@ -58,8 +58,8 @@
         return carry
 
     lax.fori_loop(1, n, greet, 0)
-    pl.semaphore_signal(barrier, inc=1, device_id={"tp": above})
-    pl.semaphore_signal(barrier, inc=1, device_id={"tp": below})
+    for d in range(1, planes):
+        pl.semaphore_signal(barrier, inc=1, device_id={"tp": lax.rem(lane + d, planes)})
 
     def remote(src, dst, sent_sem, got_sem, **to):
         return pltpu.make_async_remote_copy(src, dst, sent_sem, got_sem, device_id=to)
@@ -121,7 +121,7 @@
         return carry
 
     lax.fori_loop(0, n, pick, 0)
-    pl.semaphore_wait(barrier, n + 1)
+    pl.semaphore_wait(barrier, n + planes - 2)
 
     up_rows = upall.shape[2]
 
@@ -152,7 +152,6 @@
         )
 
     own_up = pltpu.make_async_copy(up_part(me), upall.at[me, lane], local_sem.at[1])
-    own_up.start()
 
     def begin_labels(d, carry):
         label_copy(d).start()
@@ -168,7 +167,6 @@
 
     lax.fori_loop(1, n, begin_labels, 0)
     lax.fori_loop(1, n, begin_pages, 0)
-    lax.fori_loop(1, n, begin_up, 0)
     all_labels = inlab.at[pl.ds(0, n - 1)]
     all_pages = inbox.at[pl.ds(0, (n - 1) * CAP)]
     all_up = upall.at[pl.ds(0, n - 1), 0]
@@ -207,9 +205,8 @@
         inbox, cands.at[pl.ds(page_count, n * CAP)], local_sem.at[0]
     )
     take_in.start()
-    arrived(all_up, many_got.at[2])
-    own_up.wait()
-    ring(0)
+    own_up.start()
+    lax.fori_loop(1, n, begin_up, 0)
     to_scalar.wait()
     take_in.wait()
 
@@ -382,6 +379,11 @@
         values = jnp.where(row64 + h * half == col64, values, 0.0)
         return jnp.sum(values, axis=1, keepdims=True).astype(jnp.int32)
 
+    def low_home(h, r):
+        return remote(
+            lowsend.at[h, r], lowrecv.at[h, me], low_sent.at[0, h], low_got.at[0, h], req=r
+        )
+
     def batch(h, kjs):
         for k, j in kjs:
             got_mate(h, k, j)
@@ -397,7 +399,9 @@
             part[r, whole(h)] = product[cut]
             low = jnp.where(slot_column(r, h) == 2 * me + upper, lows[cut], 0.0)
             low = low + pltpu.roll(low, rank, 1)
-            lowpart[r, h] = jnp.where(narrow, low[:quarter], low[quarter:])
+            lowsend[h, r] = jnp.where(narrow, low[:quarter], low[quarter:]).astype(jnp.bfloat16)
+            if kjs[0] != (0, 0) or i:
+                low_home(h, r).start()
 
     def batch_a(h):
         own_copy(h).wait()
@@ -413,29 +417,6 @@
 
     def target(way, step):
         return lax.rem(lane + planes + (step - hops if way == 0 else hops - step), planes)
-
-    def low_copy(h, way, step):
-        peer = below if way == 0 else above
-        src, dst = lowsend.at[h, way, step], lowrecv.at[h, way, step]
-        if step == 0:
-            some = pl.ds(way * (subs // 2), subs // 2)
-            src, dst = lowsend.at[h, way, step, some], lowrecv.at[h, way, step, some]
-        return remote(src, dst, low_sent.at[h, way, step], low_got.at[h, way, step], tp=peer)
-
-    def low_step(h, step):
-        for way in range(2):
-            if step:
-                low_copy(h, way, step - 1).wait_recv()
-            q = target(way, step)
-            for sub in range(subs):
-                mine = sub // (subs // 2) == way
-                if step == 0 and not mine:
-                    continue
-                value = lowpart[q * subs + sub, h]
-                if step > 1 or (step == 1 and mine):
-                    value = value + lowrecv[h, way, step - 1, sub].astype(jnp.float32)
-                lowsend[h, way, step, sub] = value.astype(jnp.bfloat16)
-            low_copy(h, way, step).start()
 
     wing = columns // 2
 
@@ -470,69 +451,69 @@
                     sendbuf[h, way, step, p, i] = (value + came).astype(jnp.bfloat16)
             main_copy(h, way, step, p).start()
 
-    def sum_mate():
+    home_plane = me // subs
+
+    def low_over(h):
         return remote(
-            sumsend.at[0, 1 - core], sumrecv.at[0], sum_sent.at[0], sum_got.at[0], req=mate
-        )
-
-    def sum_axis(axis, d):
-        peer = at(d, 0) if axis == 0 else at(0, d)
-        i = 1 + 3 * axis + d - 1
+            lowsum.at[h], lowz.at[h, lane], low_sent.at[1, h], low_got.at[1, h], tp=home_plane
+        )
+
+    def low_first(h):
+        arrived(lowrecv.at[h, pl.ds(0, n - 1)], low_got.at[0, h])
+        lowrecv[h, me] = lowsend[h, me]
+        value = lowrecv[h, 0].astype(jnp.float32)
+        for r in range(1, n):
+            value = value + lowrecv[h, r].astype(jnp.float32)
+        lowsum[h] = value.astype(jnp.bfloat16)
+
+        @pl.when(lane != home_plane)
+        def _():
+            low_over(h).start()
+
+    def low_spread(h, d):
+        place_of = lax.rem(me, subs)
         return remote(
-            sumsend.at[1 + axis, 0], sumrecv.at[i], sum_sent.at[i], sum_got.at[i], req=peer
-        )
-
-    def sum_back():
-        return remote(
-            lowfull.at[core], lowfull.at[core], sum_sent.at[7], sum_got.at[7], req=mate
-        )
-
-    def low_end(h):
-        for way in range(2):
-            low_copy(h, way, hops - 1).wait_recv()
+            lowfull.at[h, place_of],
+            lowfull.at[h, place_of],
+            low_sent.at[2, h],
+            full_got.at[h, place_of],
+            req=lax.rem(me + d, n),
+        )
+
+    def low_second(h):
+        @pl.when(lane == home_plane)
+        def _():
+            arrived(lowz.at[h, pl.ds(0, planes - 1)], low_got.at[1, h])
+            lowz[h, lane] = lowsum[h]
+            value = lowz[h, 0].astype(jnp.float32)
+            for t in range(1, planes):
+                value = value + lowz[h, t].astype(jnp.float32)
+            lowfull[h, lax.rem(me, subs)] = value.astype(jnp.bfloat16)
+
+            def spread(d, carry):
+                low_spread(h, d).start()
+                return carry
+
+            lax.fori_loop(1, n, spread, 0)
+
+    def lora(h):
         for sub in range(subs):
-            value = lowpart[lane * subs + sub, h]
-            for way in range(2):
-                value = value + lowrecv[h, way, hops - 1, sub].astype(jnp.float32)
-            sumsend[0, h, pl.ds(quarter * sub, quarter)] = value.astype(jnp.bfloat16)
-
-    def sum_first():
-        sum_mate().wait_recv()
-        value = sumsend[0, core].astype(jnp.float32) + sumrecv[0].astype(jnp.float32)
-        sumsend[1, 0] = value.astype(jnp.bfloat16)
-        for d in range(1, 4):
-            sum_axis(0, d).start()
-
-    def gathered(axis):
-        value = sumsend[1 + axis, 0].astype(jnp.float32)
-        for d in range(1, 4):
-            sum_axis(axis, d).wait_recv()
-            value = value + sumrecv[1 + 3 * axis + d - 1].astype(jnp.float32)
-        return value.astype(jnp.bfloat16)
-
-    def sum_second():
-        sumsend[2, 0] = gathered(0)
-        for d in range(1, 4):
-            sum_axis(1, d).start()
-
-    def sum_third():
-        lowfull[core] = gathered(1)
-        sum_back().start()
-
-    def lora():
-        arrived(lowfull.at[1 - core], sum_got.at[7])
+
+            @pl.when(lane * subs + sub != me)
+            def _():
+                arrived(lowfull.at[h, sub], full_got.at[h, sub])
+
         pieces, owners = [], []
         for sub in range(subs):
-            for h in range(HALF_COUNT):
-                packed = lowfull[h, pl.ds(quarter * sub, quarter)].astype(jnp.float32)
-                turned = pltpu.roll(packed, rank, 1)
-                pieces += [jnp.where(narrow, packed, turned), jnp.where(narrow, turned, packed)]
-                owners.append(slot_column(lane * subs + sub, h))
+            packed = lowfull[h, sub].astype(jnp.float32)
+            turned = pltpu.roll(packed, rank, 1)
+            pieces += [jnp.where(narrow, packed, turned), jnp.where(narrow, turned, packed)]
+            owners.append(slot_column(lane * subs + sub, h))
         low = jnp.concatenate(pieces, axis=0)
         owner = jnp.concatenate(owners, axis=0)
         side = lax.broadcasted_iota(jnp.int32, low.shape, 1) // rank
         group = 8
-        extra[...] = jnp.zeros(extra.shape, jnp.float32)
+        extra[h] = jnp.zeros(extra.shape[1:], jnp.float32)
 
         def add(g, carry):
             wide = jnp.concatenate(
@@ -543,18 +524,37 @@
                 axis=1,
             )
             stored = upall[pl.ds(g * group, group)].reshape(group * planes * up_rows, columns)
-            extra[...] += jnp.dot(wide, stored, preferred_element_type=jnp.float32)
+            extra[h] += jnp.dot(wide, stored, preferred_element_type=jnp.float32)
             return carry
 
         lax.fori_loop(0, n // group, add, 0)
 
+    def finish(h):
+        for sub in range(subs):
+            p, i = sub // 2, sub % 2
+            rows = pl.ds(sub * chunk_rows + h * half, half)
+            value = part[lane * subs + sub, whole(h)] + extra[h, pl.ds(sub * half, half)]
+            for way in range(2):
+                if i == 0:
+                    main_copy(h, way, hops - 1, p).wait_recv()
+                value = value + recvbuf[h, way, hops - 1, p, i].astype(jnp.float32)
+            out[rows, :] = value.astype(out.dtype)
+
+    def mains(h, step):
+        main_step(h, step, 0)
+        main_step(h, step, 1)
+
     pairs = requests // 2
-    attend(0, pairs // 2)
+    attend(0, pairs // 4)
+    arrived(all_up, many_got.at[2])
+    own_up.wait()
+    ring(0)
+    attend(pairs // 4, pairs // 2)
     open_gather(0)
-    ring(1)
     attend(pairs // 2, pairs // 2 + 2)
     near(0)
     attend(pairs // 2 + 2, pairs // 2 + 4)
+    ring(1)
     turn(0, 0)
     far(0)
     attend(pairs // 2 + 4, pairs // 2 + 6)
@@ -562,73 +562,48 @@
     turn(0, 2)
     attend(pairs // 2 + 6, pairs)
     open_gather(1)
-    ring(2)
     turn(0, 3)
     last(0, 0)
+    last(0, 1)
+    ring(2)
     batch_a(0)
-    last(0, 1)
+    batch_b(0, (0, 1))
     near(1)
-    batch_b(0, (0, 1))
-    ring(3)
     last(0, 2)
     last(0, 3)
     turn(1, 0)
+    batch_b(0, (2, 3))
     far(1)
-    batch_b(0, (2, 3))
     turn(1, 1)
+    ring(3)
     batch_c(0)
-    low_step(0, 0)
-    main_step(0, 0, 0)
-    main_step(0, 0, 1)
+    mains(0, 0)
     turn(1, 2)
-    low_step(0, 1)
-    main_step(0, 1, 0)
-    main_step(0, 1, 1)
+    batch_a(1)
     turn(1, 3)
     last(1, 0)
-    batch_a(1)
-    low_step(0, 2)
-    main_step(0, 2, 0)
+    mains(0, 1)
+    low_first(0)
     last(1, 1)
     batch_b(1, (0, 1))
-    main_step(0, 2, 1)
-    low_step(0, 3)
+    mains(0, 2)
     last(1, 2)
     last(1, 3)
     batch_b(1, (2, 3))
-    main_step(0, 3, 0)
-    main_step(0, 3, 1)
+    low_second(0)
     batch_c(1)
-    low_step(1, 0)
-    low_end(0)
-    main_step(1, 0, 0)
-    main_step(1, 0, 1)
-    low_step(1, 1)
-    main_step(1, 1, 0)
-    low_step(1, 2)
-    main_step(1, 1, 1)
-    low_step(1, 3)
-    main_step(1, 2, 0)
-    low_end(1)
-    sum_mate().start()
-    main_step(1, 2, 1)
-    sum_first()
-    main_step(1, 3, 0)
-    sum_second()
-    main_step(1, 3, 1)
-    sum_third()
+    mains(1, 0)
+    mains(0, 3)
     ring(4)
-    lora()
-    for h in range(HALF_COUNT):
-        for sub in range(subs):
-            p, i = sub // 2, sub % 2
-            rows = pl.ds(sub * chunk_rows + h * half, half)
-            value = part[lane * subs + sub, whole(h)] + extra[rows, :]
-            for way in range(2):
-                if i == 0:
-                    main_copy(h, way, hops - 1, p).wait_recv()
-                value = value + recvbuf[h, way, hops - 1, p, i].astype(jnp.float32)
-            out[rows, :] = value.astype(out.dtype)
+    lora(0)
+    mains(1, 1)
+    low_first(1)
+    finish(0)
+    mains(1, 2)
+    low_second(1)
+    mains(1, 3)
+    lora(1)
+    finish(1)
 
     arrived(all_labels, many_sent.at[0])
     arrived(all_pages, many_sent.at[1])
@@ -644,17 +619,21 @@
                 step_two(h, k, way).wait_send()
                 relay(h, k, way).wait_send()
             for step in range(hops):
-                low_copy(h, way, step).wait_send()
                 for p in range(2):
                     main_copy(h, way, step, p).wait_send()
         for k in range(4):
             for j in range(4):
                 to_mate(h, k, j).wait_send()
-    sum_mate().wait_send()
-    for axis in range(2):
-        for d in range(1, 4):
-            sum_axis(axis, d).wait_send()
-    sum_back().wait_send()
+    for h in range(HALF_COUNT):
+        arrived(lowsend.at[h, pl.ds(0, n - 1)], low_sent.at[0, h])
+
+        @pl.when(lane != home_plane)
+        def _():
+            low_over(h).wait_send()
+
+        @pl.when(lane == home_plane)
+        def _():
+            arrived(lowsend.at[h, pl.ds(0, n - 1)], low_sent.at[2, h])
 
 
 def layer(n, planes, home, adapter, storage, lengths, queries, incoming, pages, up, weights, down):
@@ -687,15 +666,14 @@
             pltpu.VMEM((n, planes, up.shape[0] // planes, columns), bf16),
             pltpu.VMEM((n, rows, depth), bf16),
             pltpu.VMEM((n, rows, columns), f32),
-            pltpu.VMEM((n, hc, half // 2, HEAD_WIDTH), f32),
             pltpu.VMEM((hc, 2, hops, 2, subs // 2, half, columns), bf16),
             pltpu.VMEM((hc, 2, hops, 2, subs // 2, half, columns), bf16),
-            pltpu.VMEM((hc, 2, hops, subs, half // 2, HEAD_WIDTH), bf16),
-            pltpu.VMEM((hc, 2, hops, subs, half // 2, HEAD_WIDTH), bf16),
-            pltpu.VMEM((3, 2, rows, HEAD_WIDTH), bf16),
-            pltpu.VMEM((7, rows, HEAD_WIDTH), bf16),
-            pltpu.VMEM((2, rows, HEAD_WIDTH), bf16),
-            pltpu.VMEM((n * rows // planes, columns), f32),
+            pltpu.VMEM((hc, n, half // 2, HEAD_WIDTH), bf16),
+            pltpu.VMEM((hc, n, half // 2, HEAD_WIDTH), bf16),
+            pltpu.VMEM((hc, half // 2, HEAD_WIDTH), bf16),
+            pltpu.VMEM((hc, planes, half // 2, HEAD_WIDTH), bf16),
+            pltpu.VMEM((hc, subs, half // 2, HEAD_WIDTH), bf16),
+            pltpu.VMEM((hc, subs * half, columns), f32),
         ]
         + [dma((3,))] * 2
         + [dma((2, hops))] * 2
@@ -704,8 +682,8 @@
         + [dma((hc, 4, 2))] * 4
         + [dma((hc, 4, 4))] * 2
         + [dma((hc, 2, hops, 2))] * 2
-        + [dma((hc, 2, hops))] * 2
-        + [dma((8,))] * 2,
+        + [dma((3, hc))] * 2
+        + [dma((hc, subs))],
         compiler_params=pltpu.CompilerParams(
             collective_id=0, has_side_effects=True, vmem_limit_bytes=VMEM_BYTES
         ),

time: 111 us -> 106 us (0.955)
  Pallas kernels: 109 us -> 103 us
    pallas_call x1, Pallas kernels: 109 us -> 103 us  [layer(): pl.pallas_call(layer_kernel, out_shape=jax.ShapeDtypeStruct((n * rows //...]
where the time goes in v5:
time: 106 us; the launch traced here: 105 us
  Pallas kernels  103 us (97%)
  local copies, waits for them, and re-layouts  1.67 us (2%)
    pallas_call x1, Pallas kernels, layer(): pl.pallas_call(layer_kernel, out_shape=jax.ShapeDtypeStruct((n * rows //...  103 us

profile of v5, /device:TPU:1, one launch (start us, length us, event | category | flops | bytes accessed | tf_op | source)
XLA Modules:
  0.0 105.1 jit_solution(1650819139898028061)
XLA Ops:
  0.0 103.5 %layer.1 = bf16[512,256]{1,0:T(8,128)(2,1)} custom-call(s32[4,128]{1,0:T(4,128)} %bitcast.9, s32[4,128]{1,0:T(4,128)} %bitcast.10, s32[32]{0:T(128)} %adapter.1, s32[64]{0:T(128)} %storage.1, s32[32]{0:T(128)} %lengths.1, bf16[128,1024]{1,0:T(8,128)(2,1)} %queries.1, bf16[2,128,128]{2,1,0:T(8,128)(2,1)} %incoming.1, bf16[512,64,128]{2,1,0:T(8,128)(2,1)} %bitcast.6, ...), custom_call_target="tpu_custom_call" | custom-call | tf_op jit(solution)/shard_map/layer/pallas_call | solution.py:649
  103.5 1.7 %copy.12 = bf16[512,256]{1,0:T(8,128)(2,1)} copy(bf16[512,256]{1,0:T(8,128)(2,1)} %layer.1) | data formatting | bytes 524288

commit v6 on v5

--- a/solution.py
+++ b/solution.py
@@ -20,7 +20,7 @@
 VMEM_BYTES = 60 * 1024 * 1024
 
 
-HALF_COUNT = 2
+HALF_COUNT = 4
 
 
 def layer_kernel(
@@ -85,7 +85,7 @@
     chosen = jnp.where(lane_of == 0, least, most)
     there = ((lane_of == 0) & (most >= 0)) | ((lane_of == 1) & (most > least))
     sourcev[...] = jnp.where(there, jnp.clip(chosen >> bits, 0, page_count - 1), 0)
-    to_sources = pltpu.make_async_copy(sourcev, sources, local_sem.at[5])
+    to_sources = pltpu.make_async_copy(sourcev, sources, local_sem.at[3 + HALF_COUNT])
     to_sources.start()
     words = jnp.where(there, ((chosen & (shift - 1)) + 1) * 64, 0)
     token_lane = lax.broadcasted_iota(jnp.int32, (1, HEAD_WIDTH), 1)
@@ -200,13 +200,13 @@
     tablev[...] = entries
     to_scalar = pltpu.make_async_copy(tablev, table, local_sem.at[2])
     to_scalar.start()
+    own_up.start()
+    lax.fori_loop(1, n, begin_up, 0)
     arrived(all_pages, many_got.at[1])
     take_in = pltpu.make_async_copy(
         inbox, cands.at[pl.ds(page_count, n * CAP)], local_sem.at[0]
     )
     take_in.start()
-    own_up.start()
-    lax.fori_loop(1, n, begin_up, 0)
     to_scalar.wait()
     take_in.wait()
 
@@ -217,15 +217,19 @@
     step_of = lax.rem(lax.broadcasted_iota(jnp.int32, (rows_q, width), 0), STEP_COUNT)
     is_key = lax.rem(column, 2) == 0
     fresh_at = column - old
-    keep_new = [
-        (fresh_at >= k * STEP_COUNT) & (fresh_at - k * STEP_COUNT <= step_of) for k in range(2)
+    places = [
+        jnp.where(
+            (fresh_at >= k * STEP_COUNT) & (fresh_at - k * STEP_COUNT <= step_of),
+            0,
+            jnp.where(is_key & (column < old), column // 2, 1 << 20),
+        )
+        for k in range(2)
     ]
-    position = jnp.where(is_key & (column < old), column // 2, 1 << 20)
-    scale = 1.0 / math.sqrt(HEAD_WIDTH)
+    scale = math.log2(math.e) / math.sqrt(HEAD_WIDTH)
     filler = jnp.zeros((HEAD_WIDTH - 4 * STEP_COUNT, HEAD_WIDTH), cands.dtype)
     per_row = HEAD_WIDTH // MAXP
 
-    def one(request, query, fresh, keep_fresh):
+    def one(request, query, fresh, position):
         pieces = []
         for j in range(MAXP):
             page = table[request // per_row, lax.rem(request, per_row) * MAXP + j]
@@ -233,17 +237,13 @@
         pieces.append(fresh)
         pieces.append(filler)
         stored = jnp.concatenate(pieces, axis=0)
-        scores = (
-            lax.dot_general(
-                query, stored, (((1,), (1,)), ((), ())), preferred_element_type=jnp.float32
-            )
-            * scale
-        )
-        keep = keep_fresh | (position < lengths[request])
-        scores = jnp.where(keep, scores, -jnp.inf)
+        scores = lax.dot_general(
+            query, stored, (((1,), (1,)), ((), ())), preferred_element_type=jnp.float32
+        )
+        scores = jnp.where(position < lengths[request], scores, -jnp.inf)
         top = jnp.max(scores, axis=1, keepdims=True)
-        exps = jnp.exp(scores - top)
-        probs = exps / jnp.sum(exps, axis=1, keepdims=True)
+        exps = jnp.exp2((scores - top) * scale)
+        probs = exps * (1.0 / jnp.sum(exps, axis=1, keepdims=True))
         probs = jnp.concatenate(
             [
                 pltpu.roll(probs[:, :old], 1, 1),
@@ -266,7 +266,7 @@
             query = jnp.concatenate(
                 [one_q[:, h * HEAD_WIDTH : (h + 1) * HEAD_WIDTH] for h in range(GROUP)], axis=0
             ).astype(jnp.bfloat16)
-            results.append(one(index * 2 + k, query, fresh, keep_new[k]))
+            results.append(one(index * 2 + k, query, fresh, places[k]))
         for h in range(GROUP):
             both = jnp.concatenate(
                 [m[h * STEP_COUNT : (h + 1) * STEP_COUNT] for m in results], axis=0
@@ -400,6 +400,7 @@
             low = jnp.where(slot_column(r, h) == 2 * me + upper, lows[cut], 0.0)
             low = low + pltpu.roll(low, rank, 1)
             lowsend[h, r] = jnp.where(narrow, low[:quarter], low[quarter:]).astype(jnp.bfloat16)
+        for i, r in enumerate(owners):
             if kjs[0] != (0, 0) or i:
                 low_home(h, r).start()
 
@@ -544,66 +545,114 @@
         main_step(h, step, 0)
         main_step(h, step, 1)
 
-    pairs = requests // 2
-    attend(0, pairs // 4)
+    def mains(h, step):
+        main_step(h, step, 0)
+        main_step(h, step, 1)
+
+    attend(0, 4)
     arrived(all_up, many_got.at[2])
     own_up.wait()
     ring(0)
-    attend(pairs // 4, pairs // 2)
     open_gather(0)
-    attend(pairs // 2, pairs // 2 + 2)
+    attend(4, 8)
     near(0)
-    attend(pairs // 2 + 2, pairs // 2 + 4)
-    ring(1)
     turn(0, 0)
+    open_gather(1)
+    attend(8, 12)
     far(0)
-    attend(pairs // 2 + 4, pairs // 2 + 6)
     turn(0, 1)
     turn(0, 2)
-    attend(pairs // 2 + 6, pairs)
-    open_gather(1)
+    ring(1)
+    near(1)
+    last(0, 0)
+    open_gather(2)
+    attend(12, 14)
+    turn(1, 0)
+    attend(14, 16)
+    last(0, 1)
+    last(0, 2)
     turn(0, 3)
-    last(0, 0)
-    last(0, 1)
-    ring(2)
+    far(1)
+    near(2)
+    turn(1, 2)
+    open_gather(3)
     batch_a(0)
     batch_b(0, (0, 1))
-    near(1)
-    last(0, 2)
+    turn(1, 1)
+    turn(2, 0)
+    last(1, 0)
+    batch_b(0, (2, 3))
     last(0, 3)
-    turn(1, 0)
-    batch_b(0, (2, 3))
-    far(1)
-    turn(1, 1)
-    ring(3)
-    batch_c(0)
-    mains(0, 0)
-    turn(1, 2)
+    ring(2)
+    far(2)
     batch_a(1)
     turn(1, 3)
-    last(1, 0)
+    near(3)
+    batch_b(1, (0, 1))
+    turn(2, 2)
+    batch_c(0)
+    last(1, 2)
+    turn(2, 1)
+    mains(0, 0)
+    batch_a(2)
+    far(3)
+    batch_b(1, (2, 3))
+    turn(3, 0)
+    last(1, 1)
+    last(2, 0)
+    turn(2, 3)
+    batch_b(2, (0, 1))
+    last(1, 3)
+    batch_a(3)
+    turn(3, 2)
+    ring(3)
+    turn(3, 1)
+    batch_b(2, (2, 3))
+    last(2, 2)
     mains(0, 1)
-    low_first(0)
-    last(1, 1)
-    batch_b(1, (0, 1))
-    mains(0, 2)
-    last(1, 2)
-    last(1, 3)
-    batch_b(1, (2, 3))
-    low_second(0)
+    last(2, 1)
     batch_c(1)
     mains(1, 0)
+    turn(3, 3)
+    last(3, 0)
+    low_first(0)
+    batch_b(3, (0, 1))
+    last(2, 3)
+    last(3, 2)
+    last(3, 1)
+    batch_b(3, (2, 3))
+    last(3, 3)
+    ring(4)
+    batch_c(2)
+    mains(2, 0)
+    mains(0, 2)
+    low_second(0)
+    mains(1, 1)
+    batch_c(3)
+    mains(3, 0)
+    mains(2, 1)
+    low_first(1)
     mains(0, 3)
-    ring(4)
+    mains(1, 2)
+    mains(3, 1)
     lora(0)
-    mains(1, 1)
-    low_first(1)
+    low_second(1)
+    low_first(2)
+    mains(2, 2)
     finish(0)
-    mains(1, 2)
-    low_second(1)
+    low_first(3)
     mains(1, 3)
+    mains(3, 2)
+    low_second(2)
+    mains(2, 3)
+    low_second(3)
     lora(1)
     finish(1)
+    mains(3, 3)
+    lora(2)
+    finish(2)
+    lora(3)
+    finish(3)
 
     arrived(all_labels, many_sent.at[0])
     arrived(all_pages, many_sent.at[1])
@@ -677,7 +726,7 @@
         ]
         + [dma((3,))] * 2
         + [dma((2, hops))] * 2
-        + [dma((6,))]
+        + [dma((4 + HALF_COUNT,))]
         + [dma((hc, 4))] * 2
         + [dma((hc, 4, 2))] * 4
         + [dma((hc, 4, 4))] * 2

time: 106 us -> 95.6 us (0.902)
  Pallas kernels: 103 us -> 93.7 us
    pallas_call x1, Pallas kernels: 103 us -> 93.7 us  [layer(): pl.pallas_call(layer_kernel, out_shape=jax.ShapeDtypeStruct((n * rows //...]
where the time goes in v6:
time: 95.6 us; the launch traced here: 95.4 us
  Pallas kernels  93.7 us (98%)
  local copies, waits for them, and re-layouts  1.67 us (2%)
    pallas_call x1, Pallas kernels, layer(): pl.pallas_call(layer_kernel, out_shape=jax.ShapeDtypeStruct((n * rows //...  93.7 us

profile of v6, /device:TPU:1, one launch (start us, length us, event | category | flops | bytes accessed | tf_op | source)
XLA Modules:
  0.0 95.4 jit_solution(18072862670052383238)
XLA Ops:
  0.0 93.7 %layer.1 = bf16[512,256]{1,0:T(8,128)(2,1)} custom-call(s32[4,128]{1,0:T(4,128)} %bitcast.9, s32[4,128]{1,0:T(4,128)} %bitcast.10, s32[32]{0:T(128)} %adapter.1, s32[64]{0:T(128)} %storage.1, s32[32]{0:T(128)} %lengths.1, bf16[128,1024]{1,0:T(8,128)(2,1)} %queries.1, bf16[2,128,128]{2,1,0:T(8,128)(2,1)} %incoming.1, bf16[512,64,128]{2,1,0:T(8,128)(2,1)} %bitcast.6, ...), custom_call_target="tpu_custom_call" | custom-call | tf_op jit(solution)/shard_map/layer/pallas_call | solution.py:698
  93.7 1.7 %copy.12 = bf16[512,256]{1,0:T(8,128)(2,1)} copy(bf16[512,256]{1,0:T(8,128)(2,1)} %layer.1) | data formatting | bytes 524288

commit v7 on v6

--- a/solution.py
+++ b/solution.py
@@ -630,28 +630,28 @@
     mains(1, 1)
     batch_c(3)
     mains(3, 0)
+    low_first(1)
     mains(2, 1)
-    low_first(1)
     mains(0, 3)
     mains(1, 2)
-    mains(3, 1)
-    lora(0)
     low_second(1)
     low_first(2)
+    mains(3, 1)
+    low_first(3)
+    lora(0)
+    finish(0)
+    low_second(2)
     mains(2, 2)
-    finish(0)
-    low_first(3)
     mains(1, 3)
+    low_second(3)
     mains(3, 2)
-    low_second(2)
     mains(2, 3)
-    low_second(3)
     lora(1)
     finish(1)
     mains(3, 3)
     lora(2)
+    lora(3)
     finish(2)
-    lora(3)
     finish(3)
 
     arrived(all_labels, many_sent.at[0])

time: 95.6 us -> 97.5 us (1.020)
  the two profiles are of different devices: /device:TPU:1 before, /device:TPU:6 now
where the time goes in v7:
time: 97.5 us; the launch traced here: 97.3 us
  Pallas kernels  95.6 us (98%)
  local copies, waits for them, and re-layouts  1.67 us (2%)
    pallas_call x1, Pallas kernels, layer(): pl.pallas_call(layer_kernel, out_shape=jax.ShapeDtypeStruct((n * rows //...  95.6 us

profile of v7, /device:TPU:6, one launch (start us, length us, event | category | flops | bytes accessed | tf_op | source)
XLA Modules:
  0.0 97.3 jit_solution(17942172618035800349)
XLA Ops:
  0.0 95.6 %layer.1 = bf16[512,256]{1,0:T(8,128)(2,1)} custom-call(s32[4,128]{1,0:T(4,128)} %bitcast.9, s32[4,128]{1,0:T(4,128)} %bitcast.10, s32[32]{0:T(128)} %adapter.1, s32[64]{0:T(128)} %storage.1, s32[32]{0:T(128)} %lengths.1, bf16[128,1024]{1,0:T(8,128)(2,1)} %queries.1, bf16[2,128,128]{2,1,0:T(8,128)(2,1)} %incoming.1, bf16[512,64,128]{2,1,0:T(8,128)(2,1)} %bitcast.6, ...), custom_call_target="tpu_custom_call" | custom-call | tf_op jit(solution)/shard_map/layer/pallas_call | solution.py:698
  95.7 1.7 %copy.12 = bf16[512,256]{1,0:T(8,128)(2,1)} copy(bf16[512,256]{1,0:T(8,128)(2,1)} %layer.1) | data formatting | bytes 524288
